TPU v7x, 32 devices: a whole 2x2x4 slice. The times are simulated.
32 devices in a mesh: rows: 8 (over y, x, core), dict: 4 (over z).
Axes of the slice: x: 2, y: 2, z: 4, core: 2. Of those that a mesh axis runs over, the one named last changes fastest.
Arguments:
- lookup_keys_per_record: int32 [131072], P(('rows', 'dict')), may hold values from 0 to 32767, as said below
- filter_passed_flags: int32 [131072], P(('rows', 'dict')), may hold values from 0 to 1
- decoding_table: bfloat16 [32768, 128], P('dict'), may hold values from -6 to 6
Outputs:
- compacted: bfloat16 [131072, 128], P(('rows', 'dict'))
Inputs may be any that keep to these rules, and one draw needn't show every extreme that they name: Codes of the rows of one device lie in one range of 8192 consecutive lookup_keys_per_record (k * 8192 to (k + 1) * 8192 - 1) at most 1365 times, and exactly 1365 times for some range, whose rows all survive.
All inputs are finite; a program needn't handle non-finite values.
Results may differ from a plain program's by a relative error of at most 0.001.
Values may be sent and summed in bfloat16 or wider, within the bound.
A program may use at most 64 MiB of HBM per device.

v0:
```python
import jax
import jax.numpy as jnp
from jax import lax
from jax.sharding import PartitionSpec as P


def prefix(shard, axis, combine, identity):
    size, mine = (lax.axis_size(axis), lax.axis_index(axis))
    everything = lax.all_gather(shard, axis)
    start = jnp.broadcast_to(jnp.asarray(identity, shard.dtype), shard.shape)

    def hop(k, before):
        reached = k < mine
        new = combine(before, everything[k])
        return jnp.where(reached, new, before)

    return lax.fori_loop(0, size, hop, start)


def from_behind(shard, axis, by):
    size = lax.axis_size(axis)
    pairs = [(i, i + by) for i in range(size) if 0 <= i + by < size]
    return lax.ppermute(shard, axis, pairs)


def summed_tallies(earlier, later):
    return earlier + later


def on_device(lookup_keys_per_record, filter_passed_flags, decoding_table):
    rows_here = lookup_keys_per_record.shape[0]
    owners = lax.axis_size("dict")
    shard = decoding_table.shape[0]
    width = decoding_table.shape[1]
    devices = lax.axis_size("rows") * lax.axis_size("dict")
    keeper_flags = filter_passed_flags > 0
    kept_tally = jnp.sum(filter_passed_flags)
    before_group = prefix(kept_tally, "dict", summed_tallies, jnp.int32(0))
    group_sum = lax.psum(kept_tally, "dict")
    before_rows = prefix(group_sum, "rows", summed_tallies, jnp.int32(0))
    beginning_offset = before_group + before_rows
    shard_inner_position = jnp.cumsum(filter_passed_flags) - 1
    owner = lookup_keys_per_record // shard
    inner = lookup_keys_per_record - owner * shard
    capacity = rows_here // min(4, owners - 1)
    one_hot_matrix = (
        (owner[:, None] == jnp.arange(owners, dtype=jnp.int32)[None, :]) & keeper_flags[:, None]
    ).astype(jnp.int32)
    slot = jnp.sum((jnp.cumsum(one_hot_matrix, axis=0) - 1) * one_hot_matrix, axis=1)
    target = jnp.where(keeper_flags, owner * capacity + slot, owners * capacity)
    requests = jnp.zeros((owners * capacity,), jnp.int32).at[target].set(inner, mode="drop")
    requests = requests.reshape(owners, 1, capacity)
    looked = jnp.take(
        decoding_table,
        lax.all_to_all(requests, "dict", split_axis=0, concat_axis=0, tiled=True)[:, 0, :],
        axis=0,
    )
    returned = lax.all_to_all(looked, "dict", split_axis=0, concat_axis=0, tiled=True)
    flat = returned.reshape(owners * capacity, width)
    picked = jnp.take(flat, jnp.minimum(target, owners * capacity - 1), axis=0)
    values = jnp.where(keeper_flags[:, None], picked, jnp.zeros_like(picked))
    device_index = lax.axis_index(("rows", "dict"))
    position = jnp.arange(rows_here, dtype=jnp.int32)
    distance = device_index * rows_here - beginning_offset + position - shard_inner_position
    tagged = jnp.where(keeper_flags, distance + 1, 0).astype(jnp.int32)
    total_bits = (devices * rows_here - 1).bit_length()
    for level in range(total_bits):
        step = 1 << level
        whole_hops, rest = divmod(step, rows_here)
        present = tagged > 0
        moving = present & (tagged - 1 >> level & 1 == 1)
        staying = present & jnp.logical_not(moving)
        send_values = jnp.where(moving[:, None], values, jnp.zeros_like(values))
        send_tags = jnp.where(moving, tagged, 0)
        if whole_hops > 0:
            far_values, far_tags = from_behind(
                (send_values, send_tags), ("rows", "dict"), -whole_hops
            )
        else:
            far_values, far_tags = (send_values, send_tags)
        if rest > 0:
            head_values, head_tags = from_behind(
                (send_values[:rest], send_tags[:rest]), ("rows", "dict"), -(whole_hops + 1)
            )
            arrived_values = jnp.concatenate([far_values[rest:], head_values], axis=0)
            arrived_tags = jnp.concatenate([far_tags[rest:], head_tags], axis=0)
        else:
            arrived_values, arrived_tags = (far_values, far_tags)
        values = jnp.where(staying[:, None], values, arrived_values)
        tagged = jnp.where(staying, tagged, arrived_tags)
    return values


def solution(mesh):
    placed = (P(("rows", "dict")), P(("rows", "dict")), P("dict", None))
    return jax.shard_map(
        on_device, mesh=mesh, in_specs=placed, out_specs=P(("rows", "dict"), None), check_vma=False
    )
```

profile of v0, /device:TPU:0, one launch (start us, length us, event | category | flops | bytes accessed | tf_op | source)
XLA Modules:
  0.0 502.4 jit_solution(3661816051059137353)
XLA Ops:
  4.2 10.6 %all-reduce.2 = (s32[4]{0:T(128)S(1)}, s32[1]{0:T(128)}) all-reduce(s32[4]{0:T(128)S(1)} %dynamic-update-slice, s32[1]{0:T(128)} %bitcast.2), channel_id=1, replica_groups=mesh['rows'=8,'dict'=4] {'dict'}, use_global_device_ids=true, to_apply=%add | all-reduce | flops 5 | bytes 40
  17.4 8.0 %all-reduce.1 = s32[8]{0:T(128)S(1)} all-reduce(s32[8]{0:T(128)S(1)} %dynamic-update-slice.1), channel_id=1, replica_groups=mesh['rows'=8,'dict'=4] {'rows'}, use_global_device_ids=true, to_apply=%add.1 | all-reduce | flops 8 | bytes 64
  25.5 10.0 %while.27 = (s32[]{:T(128)}, s32[]{:T(128)}, s32[]{:T(128)}, s32[8]{0:T(128)S(1)}, s32[]{:T(128)}) while((s32[]{:T(128)}, s32[]{:T(128)}, s32[]{:T(128)}, s32[8]{0:T(128)S(1)}, s32[]{:T(128)}) %tuple.104), condition=%wide.region_5.6_spmd, body=%wide.region_4.5_spmd.sunk | while | flops 5 | bytes 107 | solution.py:17
  35.5 5.2 %while.26 = (s32[]{:T(128)}, s32[]{:T(128)}, s32[]{:T(128)}, s32[4]{0:T(128)S(1)}, s32[]{:T(128)}) while((s32[]{:T(128)}, s32[]{:T(128)}, s32[]{:T(128)}, s32[4]{0:T(128)S(1)}, s32[]{:T(128)}) %tuple.101), condition=%wide.region_2.3_spmd, body=%wide.region_1.2_spmd.sunk | while | flops 5 | bytes 107 | solution.py:17
  52.1 15.5 %scatter_custom_fusion = s32[5460]{0:T(1024)S(1)} fusion(s32[4096]{0:T(1024)S(1)} %get-tuple-element.240, s32[4096]{0:T(1024)S(1)} %get-tuple-element.241, s32[]{:T(128)} %constant.137.clone.1), kind=kCustom, calls=%fused_computation.134 | custom fusion | bytes 21844 | tf_op jit(solution)/shard_map/scatter | solution.py:51
  78.7 12.4 %gather_fusion = bf16[5460,128]{1,0:T(8,128)(2,1)S(1)} fusion(bf16[8192,128]{1,0:T(8,128)(2,1)S(1)} %copy-done, s32[6144]{0:T(1024)} %pad_clamp_fusion), kind=kCustom, calls=%fused_computation | custom fusion | bytes 2817360 | tf_op jit(solution)/shard_map/jit(_take)/gather | solution.py:53
  96.4 4.4 all-to-all-start.1
  102.9 16.3 %collective-permute-done.2 = s32[4]{0:T(128)S(1)} collective-permute-done((s32[4]{0:T(128)S(1)}, s32[4]{0:T(128)S(1)}, u32[]{:S(2)}, u32[]{:S(2)}) %collective-permute-start.2) | collective-permute-done | bytes 48 | tf_op jit(solution)/shard_map/ppermute | solution.py:23
  121.2 18.5 %collective-permute-done.3 = s32[8]{0:T(128)S(1)} collective-permute-done((s32[8]{0:T(128)S(1)}, s32[8]{0:T(128)S(1)}, u32[]{:S(2)}, u32[]{:S(2)}) %collective-permute-start.3) | collective-permute-done | bytes 64 | tf_op jit(solution)/shard_map/ppermute | solution.py:23
  141.8 4.1 collective-permute-done.4
  147.9 4.1 collective-permute-done.5
  156.3 16.3 %gather_fusion.1 = bf16[4096,128]{1,0:T(8,128)(2,1)} fusion(bf16[5460,128]{1,0:T(8,128)(2,1)S(1)} %reshape.122, s32[4096]{0:T(1024)} %get-tuple-element.239), kind=kCustom, calls=%fused_computation.1 | custom fusion | bytes 2113536 | tf_op jit(solution)/shard_map/jit(_take)/gather | solution.py:60
  172.7 5.8 %broadcast_select_fusion.17 = bf16[4096,128]{1,0:T(8,128)(2,1)S(1)} fusion(pred[4096]{0:T(1024)(128)(4,1)S(1)} %copy-done.5, bf16[4096,128]{1,0:T(8,128)(2,1)} %gather_fusion.1, pred[4096]{0:T(1024)(128)(4,1)S(1)} %get-tuple-element.231, pred[4096]{0:T(1024)(128)(4,1)S(1)} %get-tuple-element.230), kind=kLoop, calls=%fused_computation.33 | loop fusion | flops 1572864 | bytes 2109440 | tf_op jit(solution)/shard_map/jit(_where)/select_n | solution.py:73
  184.6 4.3 broadcast_select_fusion.16
  213.6 4.3 collective-permute-done.20
  218.0 4.9 broadcast_select_fusion.12
  233.4 5.3 %collective-permute-done.22 = bf16[64,128]{1,0:T(8,128)(2,1)S(1)} collective-permute-done((bf16[64,128]{1,0:T(8,128)(2,1)S(1)}, bf16[64,128]{1,0:T(8,128)(2,1)S(1)}, u32[]{:S(2)}, u32[]{:S(2)}) %collective-permute-start.22) | collective-permute-done | bytes 16416 | tf_op jit(solution)/shard_map/ppermute | solution.py:23
  238.6 6.8 %broadcast_select_fusion.10 = (bf16[4096,128]{1,0:T(8,128)(2,1)S(1)}, bf16[4096,128]{1,0:T(8,128)(2,1)S(1)}) fusion(pred[4096]{0:T(1024)(128)(4,1)S(1)} %get-tuple-element.250, bf16[64,128]{1,0:T(8,128)(2,1)S(1)} %collective-permute-done.22, bf16[4032,128]{1,0:T(8,128)(2,1)S(1)} %slice.252, bf16[4096,128]{1,0:T(8,128)(2,1)S(1)} %get-tuple-element.216, ...), kind=kLoop, calls=%fused_computation.26 | loop fusion | flops 5767168 | bytes 5255168 | tf_op jit(solution)/shard_map/jit(_where)/select_n | solution.py:73
  248.2 4.3 collective-permute-done.23
  256.2 6.0 %collective-permute-done.24 = bf16[256,128]{1,0:T(8,128)(2,1)S(1)} collective-permute-done((bf16[256,128]{1,0:T(8,128)(2,1)S(1)}, bf16[256,128]{1,0:T(8,128)(2,1)S(1)}, u32[]{:S(2)}, u32[]{:S(2)}) %collective-permute-start.24) | collective-permute-done | bytes 65568 | tf_op jit(solution)/shard_map/ppermute | solution.py:23
  262.2 8.0 %broadcast_select_fusion.8 = (bf16[4096,128]{1,0:T(8,128)(2,1)S(1)}, bf16[4096,128]{1,0:T(8,128)(2,1)S(1)}) fusion(pred[4096]{0:T(1024)(128)(4,1)S(1)} %get-tuple-element.252, bf16[256,128]{1,0:T(8,128)(2,1)S(1)} %collective-permute-done.24, bf16[3840,128]{1,0:T(8,128)(2,1)S(1)} %slice.256, bf16[4096,128]{1,0:T(8,128)(2,1)S(1)} %get-tuple-element.210, ...), kind=kLoop, calls=%fused_computation.24 | loop fusion | flops 5767168 | bytes 5255168 | tf_op jit(solution)/shard_map/jit(_where)/select_n | solution.py:73
  271.5 6.7 %collective-permute-done.25 = bf16[512,128]{1,0:T(8,128)(2,1)S(1)} collective-permute-done((bf16[512,128]{1,0:T(8,128)(2,1)S(1)}, bf16[512,128]{1,0:T(8,128)(2,1)S(1)}, u32[]{:S(2)}, u32[]{:S(2)}) %collective-permute-start.25) | collective-permute-done | bytes 131104 | tf_op jit(solution)/shard_map/ppermute | solution.py:23
  283.8 7.0 %collective-permute-done.11 = s32[2048]{0:T(1024)S(1)} collective-permute-done((s32[2048]{0:T(1024)S(1)}, s32[2048]{0:T(1024)S(1)}, u32[]{:S(2)}, u32[]{:S(2)}) %collective-permute-start.11) | collective-permute-done | bytes 8224 | tf_op jit(solution)/shard_map/ppermute | solution.py:23
  290.9 10.4 %broadcast_select_fusion.6 = (bf16[4096,128]{1,0:T(8,128)(2,1)S(1)}, bf16[4096,128]{1,0:T(8,128)(2,1)S(1)}) fusion(pred[4096]{0:T(1024)(128)(4,1)S(1)} %get-tuple-element.254, bf16[1024,128]{1,0:T(8,128)(2,1)S(1)} %collective-permute-done.26, bf16[3072,128]{1,0:T(8,128)(2,1)S(1)} %slice.260, bf16[4096,128]{1,0:T(8,128)(2,1)S(1)} %get-tuple-element.204, ...), kind=kLoop, calls=%fused_computation.22 | loop fusion | flops 5767168 | bytes 5255168 | tf_op jit(solution)/shard_map/jit(_where)/select_n | solution.py:73
  304.0 9.8 %collective-permute-done.12 = s32[4096]{0:T(1024)S(1)} collective-permute-done((s32[4096]{0:T(1024)S(1)}, s32[4096]{0:T(1024)S(1)}, u32[]{:S(2)}, u32[]{:S(2)}) %collective-permute-start.12) | collective-permute-done | bytes 16416 | tf_op jit(solution)/shard_map/ppermute | solution.py:23
  320.3 18.3 %collective-permute-done.13 = s32[4096]{0:T(1024)S(1)} collective-permute-done((s32[4096]{0:T(1024)S(1)}, s32[4096]{0:T(1024)S(1)}, u32[]{:S(2)}, u32[]{:S(2)}) %collective-permute-start.13) | collective-permute-done | bytes 16416 | tf_op jit(solution)/shard_map/ppermute | solution.py:23
  338.6 6.4 %broadcast_select_fusion.4 = (bf16[4096,128]{1,0:T(8,128)(2,1)S(1)}, bf16[4096,128]{1,0:T(8,128)(2,1)S(1)}) fusion(pred[4096]{0:T(1024)(128)(4,1)S(1)} %get-tuple-element.256, bf16[4096,128]{1,0:T(8,128)(2,1)S(1)} %collective-permute-done.28, bf16[4096,128]{1,0:T(8,128)(2,1)S(1)} %get-tuple-element.198, bf16[2048,128]{1,0:T(8,128)(2,1)S(1)} %collective-permute-done.27, ...), kind=kLoop, calls=%fused_computation.20 | loop fusion | flops 3670016 | bytes 5255168 | tf_op jit(solution)/shard_map/jit(_where)/select_n | solution.py:73
  347.6 13.5 %collective-permute-done.14 = s32[4096]{0:T(1024)S(1)} collective-permute-done((s32[4096]{0:T(1024)S(1)}, s32[4096]{0:T(1024)S(1)}, u32[]{:S(2)}, u32[]{:S(2)}) %collective-permute-start.14) | collective-permute-done | bytes 16416 | tf_op jit(solution)/shard_map/ppermute | solution.py:23
  361.2 14.9 %collective-permute-done.29 = bf16[4096,128]{1,0:T(8,128)(2,1)S(1)} collective-permute-done((bf16[4096,128]{1,0:T(8,128)(2,1)S(1)}, bf16[4096,128]{1,0:T(8,128)(2,1)S(1)}, u32[]{:S(2)}, u32[]{:S(2)}) %collective-permute-start.29) | collective-permute-done | bytes 1048608 | tf_op jit(solution)/shard_map/ppermute | solution.py:23
  380.1 61.7 %collective-permute-done.15 = s32[4096]{0:T(1024)S(1)} collective-permute-done((s32[4096]{0:T(1024)S(1)}, s32[4096]{0:T(1024)S(1)}, u32[]{:S(2)}, u32[]{:S(2)}) %collective-permute-start.15) | collective-permute-done | bytes 16416 | tf_op jit(solution)/shard_map/ppermute | solution.py:23
  446.5 26.1 %collective-permute-done.31 = bf16[4096,128]{1,0:T(8,128)(2,1)S(1)} collective-permute-done((bf16[4096,128]{1,0:T(8,128)(2,1)S(1)}, bf16[4096,128]{1,0:T(8,128)(2,1)S(1)}, u32[]{:S(2)}, u32[]{:S(2)}) %collective-permute-start.31) | collective-permute-done | bytes 1048608 | tf_op jit(solution)/shard_map/ppermute | solution.py:23
  475.4 24.7 %collective-permute-done.32 = bf16[4096,128]{1,0:T(8,128)(2,1)S(1)} collective-permute-done((bf16[4096,128]{1,0:T(8,128)(2,1)S(1)}, bf16[4096,128]{1,0:T(8,128)(2,1)S(1)}, u32[]{:S(2)}, u32[]{:S(2)}) %collective-permute-start.32) | collective-permute-done | bytes 1048608 | tf_op jit(solution)/shard_map/ppermute | solution.py:23
  (207 shorter events, 133.9 us)
Async XLA Ops:
  44.0 5.5 %collective-permute-start = (s32[1]{0:T(128)}, s32[1]{0:T(128)}, u32[]{:S(2)}, u32[]{:S(2)}) collective-permute-start(s32[1]{0:T(128)} %slice.216), channel_id=1, source_target_pairs={{1,0},{2,1},{3,2},{4,3},{5,4},{6,5},{7,6},{8,7},{9,8},{10,9},{11,1... | collective-permute-start | bytes 20 | tf_op jit(solution)/shard_map/ppermute | solution.py:23
  68.4 9.5 %all-to-all-start = ((s32[4,1,1365]{2,1,0:T(1,128)}), s32[4,1,1365]{2,1,0:T(1,128)S(1)}, u32[]{:S(2)}, u32[]{:S(2)}) async-start(s32[4,1,1365]{2,1,0:T(1,128)} %reshape.121), calls=%async_computation | async-start | bytes 45056 | tf_op jit(solution)/shard_map/all_to_all | solution.py:55
  73.4 27.4 %collective-permute-start.1 = (s32[2]{0:T(128)}, s32[2]{0:T(128)S(1)}, u32[]{:S(2)}, u32[]{:S(2)}) collective-permute-start(s32[2]{0:T(128)} %slice.218), channel_id=1, source_target_pairs={{1,0},{2,1},{3,2},{4,3},{5,4},{6,5},{7,6},{8,7},{9,8},{10,9},{11,1... | collective-permute-start | bytes 32 | tf_op jit(solution)/shard_map/ppermute | solution.py:23
  96.4 58.1 %all-to-all-start.1 = ((bf16[4,1365,128]{2,1,0:T(8,128)(2,1)}), bf16[4,1365,128]{2,1,0:T(8,128)(2,1)}, u32[]{:S(2)}, u32[]{:S(2)}) async-start(bf16[4,1365,128]{2,1,0:T(8,128)(2,1)} %broadcast_select_fusion), calls=%async_computation.1 | async-start | bytes 2801664 | tf_op jit(solution)/shard_map/all_to_all | solution.py:58
  101.6 17.6 %collective-permute-start.2 = (s32[4]{0:T(128)S(1)}, s32[4]{0:T(128)S(1)}, u32[]{:S(2)}, u32[]{:S(2)}) collective-permute-start(s32[4]{0:T(128)S(1)} %slice.220), channel_id=1, source_target_pairs={{1,0},{2,1},{3,2},{4,3},{5,4},{6,5},{7,6},{8,7},{9,8},{10,9},{11,1... | collective-permute-start | bytes 56 | tf_op jit(solution)/shard_map/ppermute | solution.py:23
  119.9 19.8 %collective-permute-start.3 = (s32[8]{0:T(128)S(1)}, s32[8]{0:T(128)S(1)}, u32[]{:S(2)}, u32[]{:S(2)}) collective-permute-start(s32[8]{0:T(128)S(1)} %slice.222), channel_id=1, source_target_pairs={{1,0},{2,1},{3,2},{4,3},{5,4},{6,5},{7,6},{8,7},{9,8},{10,9},{11,1... | collective-permute-start | bytes 104 | tf_op jit(solution)/shard_map/ppermute | solution.py:23
  153.3 26.5 %collective-permute-start.6 = (s32[64]{0:T(128)}, s32[64]{0:T(128)}, u32[]{:S(2)}, u32[]{:S(2)}) collective-permute-start(s32[64]{0:T(128)} %slice.228), channel_id=1, source_target_pairs={{1,0},{2,1},{3,2},{4,3},{5,4},{6,5},{7,6},{8,7},{9,8},{10,9},{11,1... | collective-permute-start | bytes 776 | tf_op jit(solution)/shard_map/ppermute | solution.py:23
  178.5 6.1 %collective-permute-start.16 = (bf16[1,128]{1,0:T(2,128)(2,1)S(1)}, bf16[1,128]{1,0:T(2,128)(2,1)S(1)}, u32[]{:S(2)}, u32[]{:S(2)}) collective-permute-start(bf16[1,128]{1,0:T(2,128)(2,1)S(1)} %slice.241), channel_id=1, source_target_pairs={{1,0},{2,1},{3,2},{4,3},{5,4},{6,5},{7,6},{8,7},{9,8},{10,9},{11,1... | collective-permute-start | bytes 776 | tf_op jit(solution)/shard_map/ppermute | solution.py:23
  190.2 6.9 %collective-permute-start.7 = (s32[128]{0:T(128)S(1)}, s32[128]{0:T(128)S(1)}, u32[]{:S(2)}, u32[]{:S(2)}) collective-permute-start(s32[128]{0:T(128)S(1)} %slice.230), channel_id=1, source_target_pairs={{1,0},{2,1},{3,2},{4,3},{5,4},{6,5},{7,6},{8,7},{9,8},{10,9},{11,1... | collective-permute-start | bytes 1544 | tf_op jit(solution)/shard_map/ppermute | solution.py:23
  195.8 5.5 %collective-permute-start.18 = (bf16[4,128]{1,0:T(4,128)(2,1)S(1)}, bf16[4,128]{1,0:T(4,128)(2,1)S(1)}, u32[]{:S(2)}, u32[]{:S(2)}) collective-permute-start(bf16[4,128]{1,0:T(4,128)(2,1)S(1)} %slice.245), channel_id=1, source_target_pairs={{1,0},{2,1},{3,2},{4,3},{5,4},{6,5},{7,6},{8,7},{9,8},{10,9},{11,1... | collective-permute-start | bytes 3080 | tf_op jit(solution)/shard_map/ppermute | solution.py:23
  205.3 5.5 %collective-permute-start.19 = (bf16[8,128]{1,0:T(8,128)(2,1)S(1)}, bf16[8,128]{1,0:T(8,128)(2,1)S(1)}, u32[]{:S(2)}, u32[]{:S(2)}) collective-permute-start(bf16[8,128]{1,0:T(8,128)(2,1)S(1)} %slice.247), channel_id=1, source_target_pairs={{1,0},{2,1},{3,2},{4,3},{5,4},{6,5},{7,6},{8,7},{9,8},{10,9},{11,1... | collective-permute-start | bytes 6152 | tf_op jit(solution)/shard_map/ppermute | solution.py:23
  206.6 6.9 %collective-permute-start.8 = (s32[256]{0:T(256)S(1)}, s32[256]{0:T(256)S(1)}, u32[]{:S(2)}, u32[]{:S(2)}) collective-permute-start(s32[256]{0:T(256)S(1)} %slice.232), channel_id=1, source_target_pairs={{1,0},{2,1},{3,2},{4,3},{5,4},{6,5},{7,6},{8,7},{9,8},{10,9},{11,1... | collective-permute-start | bytes 3080 | tf_op jit(solution)/shard_map/ppermute | solution.py:23
  212.2 5.8 %collective-permute-start.20 = (bf16[16,128]{1,0:T(8,128)(2,1)S(1)}, bf16[16,128]{1,0:T(8,128)(2,1)S(1)}, u32[]{:S(2)}, u32[]{:S(2)}) collective-permute-start(bf16[16,128]{1,0:T(8,128)(2,1)S(1)} %slice.249), channel_id=1, source_target_pairs={{1,0},{2,1},{3,2},{4,3},{5,4},{6,5},{7,6},{8,7},{9,8},{10,9},{11,1... | collective-permute-start | bytes 12296 | tf_op jit(solution)/shard_map/ppermute | solution.py:23
  222.9 6.8 %collective-permute-start.21 = (bf16[32,128]{1,0:T(8,128)(2,1)S(1)}, bf16[32,128]{1,0:T(8,128)(2,1)S(1)}, u32[]{:S(2)}, u32[]{:S(2)}) collective-permute-start(bf16[32,128]{1,0:T(8,128)(2,1)S(1)} %slice.251), channel_id=1, source_target_pairs={{1,0},{2,1},{3,2},{4,3},{5,4},{6,5},{7,6},{8,7},{9,8},{10,9},{11,1... | collective-permute-start | bytes 24584 | tf_op jit(solution)/shard_map/ppermute | solution.py:23
  224.2 9.0 %collective-permute-start.9 = (s32[512]{0:T(512)S(1)}, s32[512]{0:T(512)S(1)}, u32[]{:S(2)}, u32[]{:S(2)}) collective-permute-start(s32[512]{0:T(512)S(1)} %slice.234), channel_id=1, source_target_pairs={{1,0},{2,1},{3,2},{4,3},{5,4},{6,5},{7,6},{8,7},{9,8},{10,9},{11,1... | collective-permute-start | bytes 6152 | tf_op jit(solution)/shard_map/ppermute | solution.py:23
  231.8 6.9 %collective-permute-start.22 = (bf16[64,128]{1,0:T(8,128)(2,1)S(1)}, bf16[64,128]{1,0:T(8,128)(2,1)S(1)}, u32[]{:S(2)}, u32[]{:S(2)}) collective-permute-start(bf16[64,128]{1,0:T(8,128)(2,1)S(1)} %slice.253), channel_id=1, source_target_pairs={{1,0},{2,1},{3,2},{4,3},{5,4},{6,5},{7,6},{8,7},{9,8},{10,9},{11,1... | collective-permute-start | bytes 49160 | tf_op jit(solution)/shard_map/ppermute | solution.py:23
  245.5 7.0 %collective-permute-start.23 = (bf16[128,128]{1,0:T(8,128)(2,1)S(1)}, bf16[128,128]{1,0:T(8,128)(2,1)S(1)}, u32[]{:S(2)}, u32[]{:S(2)}) collective-permute-start(bf16[128,128]{1,0:T(8,128)(2,1)S(1)} %slice.255), channel_id=1, source_target_pairs={{1,0},{2,1},{3,2},{4,3},{5,4},{6,5},{7,6},{8,7},{9,8},{10,9},{11,1... | collective-permute-start | bytes 98312 | tf_op jit(solution)/shard_map/ppermute | solution.py:23
  246.8 9.3 %collective-permute-start.10 = (s32[1024]{0:T(1024)S(1)}, s32[1024]{0:T(1024)S(1)}, u32[]{:S(2)}, u32[]{:S(2)}) collective-permute-start(s32[1024]{0:T(1024)S(1)} %slice.236), channel_id=1, source_target_pairs={{1,0},{2,1},{3,2},{4,3},{5,4},{6,5},{7,6},{8,7},{9,8},{10,9},{11,1... | collective-permute-start | bytes 12296 | tf_op jit(solution)/shard_map/ppermute | solution.py:23
  254.8 7.4 %collective-permute-start.24 = (bf16[256,128]{1,0:T(8,128)(2,1)S(1)}, bf16[256,128]{1,0:T(8,128)(2,1)S(1)}, u32[]{:S(2)}, u32[]{:S(2)}) collective-permute-start(bf16[256,128]{1,0:T(8,128)(2,1)S(1)} %slice.257), channel_id=1, source_target_pairs={{1,0},{2,1},{3,2},{4,3},{5,4},{6,5},{7,6},{8,7},{9,8},{10,9},{11,1... | collective-permute-start | bytes 196616 | tf_op jit(solution)/shard_map/ppermute | solution.py:23
  270.2 8.1 %collective-permute-start.25 = (bf16[512,128]{1,0:T(8,128)(2,1)S(1)}, bf16[512,128]{1,0:T(8,128)(2,1)S(1)}, u32[]{:S(2)}, u32[]{:S(2)}) collective-permute-start(bf16[512,128]{1,0:T(8,128)(2,1)S(1)} %slice.259), channel_id=1, source_target_pairs={{1,0},{2,1},{3,2},{4,3},{5,4},{6,5},{7,6},{8,7},{9,8},{10,9},{11,1... | collective-permute-start | bytes 393224 | tf_op jit(solution)/shard_map/ppermute | solution.py:23
  281.2 9.7 %collective-permute-start.26 = (bf16[1024,128]{1,0:T(8,128)(2,1)S(1)}, bf16[1024,128]{1,0:T(8,128)(2,1)S(1)}, u32[]{:S(2)}, u32[]{:S(2)}) collective-permute-start(bf16[1024,128]{1,0:T(8,128)(2,1)S(1)} %slice.261), channel_id=1, source_target_pairs={{1,0},{2,1},{3,2},{4,3},{5,4},{6,5},{7,6},{8,7},{9,8},{10,9},{11,1... | collective-permute-start | bytes 786440 | tf_op jit(solution)/shard_map/ppermute | solution.py:23
  282.5 8.3 %collective-permute-start.11 = (s32[2048]{0:T(1024)S(1)}, s32[2048]{0:T(1024)S(1)}, u32[]{:S(2)}, u32[]{:S(2)}) collective-permute-start(s32[2048]{0:T(1024)S(1)} %get-tuple-element.259), channel_id=1, source_target_pairs={{1,0},{2,1},{3,2},{4,3},{5,4},{6,5},{7,6},{8,7},{9,8},{10,9},{11,1... | collective-permute-start | bytes 24584 | tf_op jit(solution)/shard_map/ppermute | solution.py:23
  301.4 12.5 %collective-permute-start.27 = (bf16[2048,128]{1,0:T(8,128)(2,1)S(1)}, bf16[2048,128]{1,0:T(8,128)(2,1)S(1)}, u32[]{:S(2)}, u32[]{:S(2)}) collective-permute-start(bf16[2048,128]{1,0:T(8,128)(2,1)S(1)} %get-tuple-element.234), channel_id=1, source_target_pairs={{1,0},{2,1},{3,2},{4,3},{5,4},{6,5},{7,6},{8,7},{9,8},{10,9},{11,1... | collective-permute-start | bytes 1572872 | tf_op jit(solution)/shard_map/ppermute | solution.py:23
  302.7 11.1 %collective-permute-start.12 = (s32[4096]{0:T(1024)S(1)}, s32[4096]{0:T(1024)S(1)}, u32[]{:S(2)}, u32[]{:S(2)}) collective-permute-start(s32[4096]{0:T(1024)S(1)} %broadcast_select_fusion.26), channel_id=1, source_target_pairs={{1,0},{2,1},{3,2},{4,3},{5,4},{6,5},{7,6},{8,7},{9,8},{10,9},{11,1... | collective-permute-start | bytes 49160 | tf_op jit(solution)/shard_map/ppermute | solution.py:23
  317.7 20.9 %collective-permute-start.28 = (bf16[4096,128]{1,0:T(8,128)(2,1)S(1)}, bf16[4096,128]{1,0:T(8,128)(2,1)S(1)}, u32[]{:S(2)}, u32[]{:S(2)}) collective-permute-start(bf16[4096,128]{1,0:T(8,128)(2,1)S(1)} %broadcast_select_fusion.5), channel_id=1, source_target_pairs={{1,0},{2,1},{3,2},{4,3},{5,4},{6,5},{7,6},{8,7},{9,8},{10,9},{11,1... | collective-permute-start | bytes 3145736 | tf_op jit(solution)/shard_map/ppermute | solution.py:23
  319.0 19.6 %collective-permute-start.13 = (s32[4096]{0:T(1024)S(1)}, s32[4096]{0:T(1024)S(1)}, u32[]{:S(2)}, u32[]{:S(2)}) collective-permute-start(s32[4096]{0:T(1024)S(1)} %broadcast_select_fusion.25), channel_id=1, source_target_pairs={{2,0},{3,1},{4,2},{5,3},{6,4},{7,5},{8,6},{9,7},{10,8},{11,9},{12,... | collective-permute-start | bytes 49160 | tf_op jit(solution)/shard_map/ppermute | solution.py:23
  345.0 31.1 %collective-permute-start.29 = (bf16[4096,128]{1,0:T(8,128)(2,1)S(1)}, bf16[4096,128]{1,0:T(8,128)(2,1)S(1)}, u32[]{:S(2)}, u32[]{:S(2)}) collective-permute-start(bf16[4096,128]{1,0:T(8,128)(2,1)S(1)} %get-tuple-element.191), channel_id=1, source_target_pairs={{2,0},{3,1},{4,2},{5,3},{6,4},{7,5},{8,6},{9,7},{10,8},{11,9},{12,... | collective-permute-start | bytes 3145736 | tf_op jit(solution)/shard_map/ppermute | solution.py:23
  346.3 14.8 %collective-permute-start.14 = (s32[4096]{0:T(1024)S(1)}, s32[4096]{0:T(1024)S(1)}, u32[]{:S(2)}, u32[]{:S(2)}) collective-permute-start(s32[4096]{0:T(1024)S(1)} %broadcast_select_fusion.24), channel_id=1, source_target_pairs={{4,0},{5,1},{6,2},{7,3},{8,4},{9,5},{10,6},{11,7},{12,8},{13,9},{1... | collective-permute-start | bytes 49160 | tf_op jit(solution)/shard_map/ppermute | solution.py:23
  377.5 64.4 %collective-permute-start.30 = (bf16[4096,128]{1,0:T(8,128)(2,1)S(1)}, bf16[4096,128]{1,0:T(8,128)(2,1)S(1)}, u32[]{:S(2)}, u32[]{:S(2)}) collective-permute-start(bf16[4096,128]{1,0:T(8,128)(2,1)S(1)} %broadcast_select_fusion.3), channel_id=1, source_target_pairs={{4,0},{5,1},{6,2},{7,3},{8,4},{9,5},{10,6},{11,7},{12,8},{13,9},{1... | collective-permute-start | bytes 3145736 | tf_op jit(solution)/shard_map/ppermute | solution.py:23
  378.8 63.0 %collective-permute-start.15 = (s32[4096]{0:T(1024)S(1)}, s32[4096]{0:T(1024)S(1)}, u32[]{:S(2)}, u32[]{:S(2)}) collective-permute-start(s32[4096]{0:T(1024)S(1)} %broadcast_select_fusion.23), channel_id=1, source_target_pairs={{8,0},{9,1},{10,2},{11,3},{12,4},{13,5},{14,6},{15,7},{16,8},{17,9... | collective-permute-start | bytes 49160 | tf_op jit(solution)/shard_map/ppermute | solution.py:23
  445.2 27.4 %collective-permute-start.31 = (bf16[4096,128]{1,0:T(8,128)(2,1)S(1)}, bf16[4096,128]{1,0:T(8,128)(2,1)S(1)}, u32[]{:S(2)}, u32[]{:S(2)}) collective-permute-start(bf16[4096,128]{1,0:T(8,128)(2,1)S(1)} %get-tuple-element.185), channel_id=1, source_target_pairs={{8,0},{9,1},{10,2},{11,3},{12,4},{13,5},{14,6},{15,7},{16,8},{17,9... | collective-permute-start | bytes 3145736 | tf_op jit(solution)/shard_map/ppermute | solution.py:23
  474.1 26.0 %collective-permute-start.32 = (bf16[4096,128]{1,0:T(8,128)(2,1)S(1)}, bf16[4096,128]{1,0:T(8,128)(2,1)S(1)}, u32[]{:S(2)}, u32[]{:S(2)}) collective-permute-start(bf16[4096,128]{1,0:T(8,128)(2,1)S(1)} %broadcast_select_fusion.1), channel_id=1, source_target_pairs={{16,0},{17,1},{18,2},{19,3},{20,4},{21,5},{22,6},{23,7},{24,8},{25... | collective-permute-start | bytes 3145736 | tf_op jit(solution)/shard_map/ppermute | solution.py:23
  (16 other events, 199.8 us)
where the time goes:
time: 505 us; the launch traced here: 502 us
  waiting for transfers between devices  267 us (53%)
  other arithmetic  90.9 us (18%)
  local copies, waits for them, and re-layouts  65.5 us (13%)
  starting transfers between devices  51.1 us (10%)
  blocking collectives  18.6 us (4%)
  loops' own time  7.95 us (2%)
    ppermute x33, waiting for transfers between devices, from_behind(): return lax.ppermute(shard, axis, pairs)  264 us
    select_n x17, other arithmetic, on_device(): send_values = jnp.where(moving[:, None], values, jnp.zeros_like(values))  70.6 us
    ppermute x33, starting transfers between devices, from_behind(): return lax.ppermute(shard, axis, pairs)  42.8 us
    unnamed x2, blocking collectives  18.6 us
    gather x1, local copies, waits for them, and re-layouts, on_device(): picked = jnp.take(flat, jnp.minimum(target, owners * capacity - 1), axis=0)  16.3 us
    scatter x1, local copies, waits for them, and re-layouts, on_device(): jnp.zeros((owners * capacity,), jnp.int32).at[target]  15.5 us
    gather x2, local copies, waits for them, and re-layouts, on_device(): jnp.take(decoding_table, lax.all_to_all(requests, 'dict', split_axis=0, c...  13.9 us
  transfers between devices with their start and end apart: 35, of which 24 were waited for; matrix products, arithmetic and copies ran while one was open for 12% of the time, Pallas kernels for 0%

commit v1 on v0

v1 whole, which is shorter than its diff:
```python
import functools

import jax
import jax.numpy as jnp
from jax import lax
from jax.experimental import pallas as pl
from jax.experimental.pallas import tpu as pltpu
from jax.sharding import PartitionSpec as P

LANES = 128


def shifted_left(x, step, lane):
    rows = x.shape[0]
    whole, rest = divmod(step, LANES)
    here = pltpu.roll(x, (rows - whole) % rows, 0) if whole % rows else x
    if rest == 0:
        return here
    above = pltpu.roll(here, rows - 1, 0) if rows > 1 else here
    return jnp.where(
        lane < LANES - rest,
        pltpu.roll(here, LANES - rest, 1),
        pltpu.roll(above, LANES - rest, 1),
    )


def running_sum(x, lane, row):
    rows = x.shape[0]
    total = x
    step = 1
    while step < LANES:
        total = total + jnp.where(lane >= step, pltpu.roll(total, step, 1), 0)
        step *= 2
    ends = jnp.broadcast_to(total[:, LANES - 1 :], x.shape)
    before = jnp.where(row >= 1, pltpu.roll(ends, 1, 0), 0)
    step = 1
    while step < rows:
        before = before + jnp.where(row >= step, pltpu.roll(before, step, 0), 0)
        step *= 2
    return total + before


def compact_kernel(codes_ref, flags_ref, out_ref):
    rows = codes_ref.shape[0]
    lane = lax.broadcasted_iota(jnp.int32, (rows, LANES), 1)
    row = lax.broadcasted_iota(jnp.int32, (rows, LANES), 0)
    kept = flags_ref[...] > 0
    sums = running_sum(kept.astype(jnp.int32), lane, row)
    position = row * LANES + lane
    tags = jnp.where(kept, position - sums + 2, 0)
    values = codes_ref[...]
    step = 1
    level = 0
    while step < rows * LANES:
        moving = (tags > 0) & (((tags - 1) >> level) & 1 == 1)
        arrived_tags = shifted_left(jnp.where(moving, tags, 0), step, lane)
        arrived_values = shifted_left(values, step, lane)
        arrives = (arrived_tags > 0) & (position < rows * LANES - step)
        values = jnp.where(arrives, arrived_values, values)
        tags = jnp.where(arrives, arrived_tags, jnp.where(moving, 0, tags))
        step *= 2
        level += 1
    out_ref[:rows, :] = values
    total = jnp.broadcast_to(sums[rows - 1 :, LANES - 1 :], (8, LANES))
    out_ref[rows:, :] = total


def pick_kernel(me_ref, counts_ref, codes_ref, out_ref):
    blocks = codes_ref.shape[0]
    rows = codes_ref.shape[1] - 8
    size = rows * LANES
    lane = lax.broadcasted_iota(jnp.int32, (rows, LANES), 1)
    row = lax.broadcasted_iota(jnp.int32, (rows, LANES), 0)
    position = row * LANES + lane
    out_ref[...] = jnp.full((rows, LANES), -1, jnp.int32)
    first = me_ref[0] * size

    def source(s, start):
        count = counts_ref[s]
        begin = start - first

        @pl.when((begin < size) & (begin + count > 0))
        def _():
            shift = lax.rem(begin + size, size)
            by_row = shift // LANES
            by_lane = lax.rem(shift, LANES)
            moved = pltpu.roll(codes_ref[s, :rows, :], by_row, 0)
            below = pltpu.roll(moved, 1, 0)
            picked = jnp.where(
                lane >= by_lane, pltpu.roll(moved, by_lane, 1), pltpu.roll(below, by_lane, 1)
            )
            inside = (position >= begin) & (position < begin + count)
            out_ref[...] = jnp.where(inside, picked, out_ref[...])

        return start + count

    lax.fori_loop(0, blocks, source, jnp.int32(0))


def on_device(lookup_keys_per_record, filter_passed_flags, decoding_table):
    rows_here = lookup_keys_per_record.shape[0]
    shard, width = decoding_table.shape
    groups = lax.axis_size("rows")
    rows = rows_here // LANES
    vmem = pl.BlockSpec(memory_space=pltpu.VMEM)
    smem = pl.BlockSpec(memory_space=pltpu.SMEM)

    part = shard // groups
    mine = lax.dynamic_slice_in_dim(decoding_table, lax.axis_index("rows") * part, part, 0)
    table = lax.all_gather(mine, ("dict", "rows"), tiled=True)

    compacted = pl.pallas_call(
        compact_kernel,
        out_shape=jax.ShapeDtypeStruct((rows + 8, LANES), jnp.int32),
        in_specs=[vmem, vmem],
        out_specs=vmem,
    )(lookup_keys_per_record.reshape(rows, LANES), filter_passed_flags.reshape(rows, LANES))
    everyone = lax.all_gather(compacted, ("rows", "dict"))
    counts = everyone[:, rows, 0]
    me = lax.axis_index(("rows", "dict")).astype(jnp.int32).reshape(1)
    codes = pl.pallas_call(
        pick_kernel,
        out_shape=jax.ShapeDtypeStruct((rows, LANES), jnp.int32),
        in_specs=[smem, smem, vmem],
        out_specs=vmem,
    )(me, counts, everyone).reshape(rows_here)
    picked = jnp.take(table, jnp.maximum(codes, 0), axis=0, mode="clip")
    return jnp.where((codes >= 0)[:, None], picked, jnp.zeros_like(picked))


def solution(mesh):
    placed = (P(("rows", "dict")), P(("rows", "dict")), P("dict", None))
    return jax.shard_map(
        on_device, mesh=mesh, in_specs=placed, out_specs=P(("rows", "dict"), None), check_vma=False
    )
```

time: 505 us -> 124 us (0.25)
  waiting for transfers between devices: 267 us -> 0.02 us
  other arithmetic: 90.9 us -> 4.33 us
  blocking collectives: 18.6 us -> 81.8 us
  starting transfers between devices: 51.1 us -> 0.01 us
  local copies, waits for them, and re-layouts: 65.5 us -> 19.1 us
  between operations: 1.03 us -> 13.4 us
  loops' own time: 7.95 us -> 0 us
    ppermute x33 -> x0, waiting for transfers between devices: 264 us -> none  [from_behind(): return lax.ppermute(shard, axis, pairs)]
    all_gather x0 -> x1, blocking collectives: none -> 81.8 us  [on_device(): everyone = lax.all_gather(compacted, ('rows', 'dict'))]
    select_n x36 -> x1, other arithmetic: 77.2 us -> 2.88 us  [on_device(): return jnp.where((codes >= 0)[:, None], picked, jnp.zeros_like(picked))]
    ppermute x33 -> x0, starting transfers between devices: 42.8 us -> none  [from_behind(): return lax.ppermute(shard, axis, pairs)]
    unnamed x2 -> x0, blocking collectives: 18.6 us -> none
    scatter x1 -> x0, local copies, waits for them, and re-layouts: 15.5 us -> none  [on_device(): jnp.zeros((owners * capacity,), jnp.int32).at[target]]
    gather x3 -> x1, local copies, waits for them, and re-layouts: 30.2 us -> 15.5 us  [on_device(): picked = jnp.take(table, jnp.maximum(codes, 0), axis=0, mode='clip')]
    all_to_all x2 -> x0, starting transfers between devices: 8.31 us -> none  [the longest x1 4.44 us: on_device(): lax.all_to_all(looked, 'dict', split_axis=0, concat_axis=0, tiled=True)]
  transfers between devices with their start and end apart: 35 -> 1, of which waited for: 24 -> 0; matrix products, arithmetic and copies ran while one was open for 12% -> 2% of each run, Pallas kernels for 0% -> 4%
where the time goes in v1:
time: 124 us
  blocking collectives  81.8 us (66%)
  local copies, waits for them, and re-layouts  19.1 us (15%)
  between operations  13.4 us (11%)
  Pallas kernels  4.89 us (4%)
  other arithmetic  4.33 us (3%)
    all_gather x1, blocking collectives, on_device(): everyone = lax.all_gather(compacted, ('rows', 'dict'))  81.8 us
    gather x1, local copies, waits for them, and re-layouts, on_device(): picked = jnp.take(table, jnp.maximum(codes, 0), axis=0, mode='clip')  15.5 us
    select_n x1, other arithmetic, on_device(): return jnp.where((codes >= 0)[:, None], picked, jnp.zeros_like(picked))  2.88 us
    pallas_call x1, Pallas kernels, on_device(): pl.pallas_call(compact_kernel, out_shape=jax.ShapeDtypeStruct((rows + 8,...  2.55 us
  transfers between devices with their start and end apart: 1, of which 0 were waited for; matrix products, arithmetic and copies ran while one was open for 2% of the time, Pallas kernels for 4%

profile of v1, /device:TPU:0, one launch (start us, length us, event | category | flops | bytes accessed | tf_op | source)
XLA Modules:
  0.0 123.5 jit_solution(17388499480168148820)
XLA Ops:
  6.5 0.0 copy-start
  6.5 0.0 all-gather.3.cloned.1.call-start
  6.5 1.6 %copy-done = bf16[8192,128]{1,0:T(8,128)(2,1)S(1)} copy-done((bf16[8192,128]{1,0:T(8,128)(2,1)S(1)}, bf16[8192,128]{1,0:T(8,128)(2,1)}, u32[]{:S(2)}) %copy-start) | copy-done | bytes 2097176
  8.1 0.7 constant_dynamic-slice_fusion
  8.9 0.0 all-gather.3.cloned.1.call-update
  8.9 2.5 %shard_map.37 = s32[40,128]{1,0:T(8,128)} custom-call(s32[32,128]{1,0:T(8,128)} %bitcast.10, s32[32,128]{1,0:T(8,128)} %bitcast.11), custom_call_target="tpu_custom_call" | custom-call | tf_op jit(solution)/shard_map/pallas_call | solution.py:112
  11.4 81.8 %all-gather = s32[1280,128]{1,0:T(8,128)S(1)} all-gather(s32[40,128]{1,0:T(8,128)} %shard_map.37), channel_id=2, replica_groups=mesh['rows'=8,'dict'=4] {'rows','dict'}, dimensions={0}, use_global_device_ids=true | all-gather | bytes 675840 | tf_op jit(solution)/shard_map/all_gather | solution.py:118
  93.3 0.0 copy-start.1
  93.3 1.3 %slice_reduce_fusion.counts_ref = s32[32]{0:T(128)} fusion(s32[32,40,128]{2,1,0:T(8,128)S(1)} %bitcast.8), kind=kLoop, calls=%fused_computation.2 | loop fusion | bytes 256 | tf_op jit(solution)/shard_map/slice | solution.py:119
  94.5 0.0 copy-done.1
  94.5 2.3 %shard_map.38 = s32[32,128]{1,0:T(8,128)} custom-call(s32[1]{0:T(128)} %bitcast.me_ref, s32[32]{0:T(128)} %slice_reduce_fusion.counts_ref, s32[32,40,128]{2,1,0:T(8,128)} %bitcast.9), custom_call_target="tpu_custom_call" | custom-call | tf_op jit(solution)/shard_map/pallas_call | solution.py:121
  96.9 0.7 compare_bitcast_fusion
  97.6 0.7 bitcast_clamp_fusion
  98.3 0.0 all-gather.3.cloned.1.call-done
  98.3 15.5 %gather_fusion = bf16[4096,128]{1,0:T(8,128)(2,1)S(1)} fusion(bf16[32768,128]{1,0:T(8,128)(2,1)} %all-gather.3.cloned.1.call-done, s32[4096]{0:T(1024)S(1)} %bitcast_clamp_fusion), kind=kCustom, calls=%fused_computation | custom fusion | bytes 2113536 | tf_op jit(solution)/shard_map/jit(_take)/gather | solution.py:127
  113.8 2.9 %broadcast_select_fusion = bf16[4096,128]{1,0:T(8,128)(2,1)} fusion(bf16[4096,128]{1,0:T(8,128)(2,1)S(1)} %gather_fusion, pred[4096]{0:T(1024)(128)(4,1)S(1)} %compare_bitcast_fusion), kind=kLoop, calls=%fused_computation.1 | loop fusion | flops 524288 | bytes 2101248 | tf_op jit(solution)/shard_map/jit(_where)/select_n | solution.py:128
Async XLA Ops:
  6.5 1.6 %copy-start = (bf16[8192,128]{1,0:T(8,128)(2,1)S(1)}, bf16[8192,128]{1,0:T(8,128)(2,1)}, u32[]{:S(2)}) copy-start(bf16[8192,128]{1,0:T(8,128)(2,1)} %param.5) | copy-start | bytes 6291460
  6.5 91.8 %all-gather.3.cloned.1.call-start = ((), (), s32[]{:S(2)}) async-start(), calls=%async_computation | async-start | bytes 8650752 | tf_op jit(solution)/shard_map/all_gather | solution.py:110
  93.3 1.3 %copy-start.1 = (s32[1280,128]{1,0:T(8,128)}, s32[1280,128]{1,0:T(8,128)S(1)}, u32[]{:S(2)}) copy-start(s32[1280,128]{1,0:T(8,128)S(1)} %all-gather) | copy-start | bytes 1966084
Sparse Core Ops, SparseCore 0:
  10.2 83.4 all-gather.2

commit v2 on v1

--- a/solution.py
+++ b/solution.py
@@ -97,17 +97,142 @@
     lax.fori_loop(0, blocks, source, jnp.int32(0))
 
 
+def forwarding(groups):
+    bits = [1 << k for k in range(groups.bit_length() - 1)]
+    return (bits[1:] + bits[:1], bits[:0:-1] + bits[:1])
+
+
+def arrivals(order):
+    arrived = [(0, -1)]
+    for k, bit in enumerate(order):
+        arrived += [(e ^ bit, k) for e, _ in arrived]
+    return arrived
+
+
+def table_kernel(groups, owners, shard_ref, out_ref, dict_send, dict_recv, send, recv, local):
+    r = lax.axis_index("rows")
+    z = lax.axis_index("dict")
+    shard = shard_ref.shape[0]
+    part = shard // groups
+    half = part // 2
+    orders = forwarding(groups)
+    stages = [arrivals(order) for order in orders]
+
+    def plane(peer):
+        return {"rows": peer}
+
+    def column(peer):
+        return {"dict": peer}
+
+    barrier = pltpu.get_barrier_semaphore()
+    greeted = 0
+    for d in range(1, owners):
+        pl.semaphore_signal(
+            barrier, inc=1, device_id=column(lax.rem(z + d, owners)), device_id_type=pl.DeviceIdType.MESH
+        )
+        greeted += 1
+    for bit in orders[0]:
+        pl.semaphore_signal(
+            barrier, inc=1, device_id=plane(flipped(r, bit)), device_id_type=pl.DeviceIdType.MESH
+        )
+        greeted += 1
+    pl.semaphore_wait(barrier, greeted)
+
+    def place(owner, group, start, size):
+        at = owner * shard + group * part + start
+        return pl.ds(pl.multiple_of(at, half), size)
+
+    nearest = sorted(range(1, owners), key=lambda d: min(d, owners - d))
+    sent = []
+    for d in nearest:
+        copy = pltpu.make_async_remote_copy(
+            src_ref=shard_ref.at[pl.ds(pl.multiple_of(r * part, part), part)],
+            dst_ref=out_ref.at[place(z, r, 0, part)],
+            send_sem=dict_send.at[d - 1],
+            recv_sem=dict_recv.at[d - 1],
+            device_id=column(lax.rem(z + d, owners)),
+            device_id_type=pl.DeviceIdType.MESH,
+        )
+        copy.start()
+        sent.append(copy)
+    own = pltpu.make_async_copy(
+        shard_ref, out_ref.at[pl.ds(pl.multiple_of(z * shard, shard), shard)], local.at[0]
+    )
+    own.start()
+
+    received = {}
+    first = {d: sent[i] for i, d in enumerate(nearest)}
+    for index in range(groups):
+        for d in nearest:
+            owner = lax.rem(z + owners - d, owners)
+            if index == 0:
+                first[d].wait_recv()
+            for h in range(2):
+                offset, k = stages[h][index]
+                if index > 0:
+                    received[d, h, offset].wait_recv()
+                where = place(owner, flipped(r, offset), h * half, half)
+                for later in range(k + 1, len(orders[h])):
+                    bit = orders[h][later]
+                    lane = ((d - 1) * 2 + h) * groups + (offset ^ bit)
+                    copy = pltpu.make_async_remote_copy(
+                        src_ref=out_ref.at[where],
+                        dst_ref=out_ref.at[where],
+                        send_sem=send.at[lane],
+                        recv_sem=recv.at[lane],
+                        device_id=plane(flipped(r, bit)),
+                        device_id_type=pl.DeviceIdType.MESH,
+                    )
+                    copy.start()
+                    sent.append(copy)
+                    received[d, h, offset ^ bit] = copy
+    for copy in sent:
+        copy.wait_send()
+    own.wait()
+
+
+def flipped(r, mask):
+    out = r
+    bit = 1
+    while bit <= mask:
+        if mask & bit:
+            out = out + bit - 2 * bit * lax.rem(lax.div(r, bit), 2)
+        bit *= 2
+    return out
+
+
+def gathered_table(decoding_table):
+    groups = lax.axis_size("rows")
+    owners = lax.axis_size("dict")
+    shard, width = decoding_table.shape
+    flights = (owners - 1) * 2 * groups
+    return pl.pallas_call(
+        functools.partial(table_kernel, groups, owners),
+        out_shape=jax.ShapeDtypeStruct((owners * shard, width), decoding_table.dtype),
+        in_specs=[pl.BlockSpec(memory_space=pltpu.VMEM)],
+        out_specs=pl.BlockSpec(memory_space=pl.ANY),
+        scratch_shapes=[
+            pltpu.SemaphoreType.DMA((owners - 1,)),
+            pltpu.SemaphoreType.DMA((owners - 1,)),
+            pltpu.SemaphoreType.DMA((flights,)),
+            pltpu.SemaphoreType.DMA((flights,)),
+            pltpu.SemaphoreType.DMA((1,)),
+        ],
+        compiler_params=pltpu.CompilerParams(collective_id=0, has_side_effects=True),
+        cost_estimate=pl.CostEstimate(
+            flops=0, bytes_accessed=16 * owners * shard * width, transcendentals=0
+        ),
+    )(decoding_table)
+
+
 def on_device(lookup_keys_per_record, filter_passed_flags, decoding_table):
     rows_here = lookup_keys_per_record.shape[0]
     shard, width = decoding_table.shape
-    groups = lax.axis_size("rows")
     rows = rows_here // LANES
     vmem = pl.BlockSpec(memory_space=pltpu.VMEM)
     smem = pl.BlockSpec(memory_space=pltpu.SMEM)
 
-    part = shard // groups
-    mine = lax.dynamic_slice_in_dim(decoding_table, lax.axis_index("rows") * part, part, 0)
-    table = lax.all_gather(mine, ("dict", "rows"), tiled=True)
+    table = gathered_table(decoding_table)
 
     compacted = pl.pallas_call(
         compact_kernel,

time: 124 us -> 144 us (1.16)
  Pallas kernels: 4.89 us -> 46.8 us
  between operations: 13.4 us -> 0.02 us
  blocking collectives: 81.8 us -> 75.4 us
  local copies, waits for them, and re-layouts: 19.1 us -> 16.7 us
    pallas_call x0 -> x1, Pallas kernels: none -> 42 us  [gathered_table(): pl.pallas_call(functools.partial(table_kernel, groups, owners), out_shape...]
    all_gather x1, blocking collectives: 81.8 us -> 75.4 us  [on_device(): everyone = lax.all_gather(compacted, ('rows', 'dict'))]
    unnamed x4 -> x2, local copies, waits for them, and re-layouts: 1.59 us -> 0.01 us
  transfers between devices with their start and end apart: 1 -> 0, of which waited for: 0 -> 0; matrix products, arithmetic and copies ran while one was open for 2% -> 0% of each run, Pallas kernels for 4% -> 0%
where the time goes in v2:
time: 144 us; the launch traced here: 143 us
  blocking collectives  75.4 us (52%)
  Pallas kernels  46.8 us (32%)
  local copies, waits for them, and re-layouts  16.7 us (12%)
  other arithmetic  4.33 us (3%)
    all_gather x1, blocking collectives, on_device(): everyone = lax.all_gather(compacted, ('rows', 'dict'))  75.4 us
    pallas_call x1, Pallas kernels, gathered_table(): pl.pallas_call(functools.partial(table_kernel, groups, owners), out_shape...  42 us
    gather x1, local copies, waits for them, and re-layouts, on_device(): picked = jnp.take(table, jnp.maximum(codes, 0), axis=0, mode='clip')  15.5 us
    select_n x1, other arithmetic, on_device(): return jnp.where((codes >= 0)[:, None], picked, jnp.zeros_like(picked))  2.88 us

profile of v2, /device:TPU:0, one launch (start us, length us, event | category | flops | bytes accessed | tf_op | source)
XLA Modules:
  0.0 143.2 jit_solution(5291573644708821589)
XLA Ops:
  0.0 2.5 %shard_map.37 = s32[40,128]{1,0:T(8,128)} custom-call(s32[32,128]{1,0:T(8,128)} %bitcast.10, s32[32,128]{1,0:T(8,128)} %bitcast.11), custom_call_target="tpu_custom_call" | custom-call | tf_op jit(solution)/shard_map/pallas_call | solution.py:237
  2.5 75.4 %all-gather = s32[1280,128]{1,0:T(8,128)S(1)} all-gather(s32[40,128]{1,0:T(8,128)} %shard_map.37), channel_id=2, replica_groups=mesh['rows'=8,'dict'=4] {'rows','dict'}, dimensions={0}, use_global_device_ids=true | all-gather | bytes 675840 | tf_op jit(solution)/shard_map/all_gather | solution.py:243
  77.9 0.0 copy-start
  77.9 1.2 slice_reduce_fusion.counts_ref
  79.1 0.0 copy-done
  79.1 2.3 %shard_map.38 = s32[32,128]{1,0:T(8,128)} custom-call(s32[1]{0:T(128)} %bitcast.me_ref, s32[32]{0:T(128)} %slice_reduce_fusion.counts_ref, s32[32,40,128]{2,1,0:T(8,128)} %bitcast.9), custom_call_target="tpu_custom_call" | custom-call | tf_op jit(solution)/shard_map/pallas_call | solution.py:246
  81.4 0.7 compare_bitcast_fusion
  82.1 0.7 bitcast_clamp_fusion
  82.8 42.0 %shard_map.39 = bf16[32768,128]{1,0:T(8,128)(2,1)} custom-call(bf16[8192,128]{1,0:T(8,128)(2,1)} %shard_ref.1), custom_call_target="tpu_custom_call" | custom-call | bytes 67108864 | tf_op jit(solution)/shard_map/pallas_call | solution.py:209
  124.8 15.5 %gather_fusion = bf16[4096,128]{1,0:T(8,128)(2,1)S(1)} fusion(bf16[32768,128]{1,0:T(8,128)(2,1)} %shard_map.39, s32[4096]{0:T(1024)S(1)} %bitcast_clamp_fusion), kind=kCustom, calls=%fused_computation | custom fusion | bytes 2113536 | tf_op jit(solution)/shard_map/jit(_take)/gather | solution.py:252
  140.3 2.9 %broadcast_select_fusion = bf16[4096,128]{1,0:T(8,128)(2,1)} fusion(bf16[4096,128]{1,0:T(8,128)(2,1)S(1)} %gather_fusion, pred[4096]{0:T(1024)(128)(4,1)S(1)} %compare_bitcast_fusion), kind=kLoop, calls=%fused_computation.1 | loop fusion | flops 524288 | bytes 2101248 | tf_op jit(solution)/shard_map/jit(_where)/select_n | solution.py:253
Async XLA Ops:
  77.9 1.2 copy-start

commit v3 on v2

--- a/solution.py
+++ b/solution.py
@@ -65,14 +65,14 @@
     out_ref[rows:, :] = total
 
 
-def pick_kernel(me_ref, counts_ref, codes_ref, out_ref):
+def pick_kernel(blank, me_ref, counts_ref, codes_ref, out_ref):
     blocks = codes_ref.shape[0]
     rows = codes_ref.shape[1] - 8
     size = rows * LANES
     lane = lax.broadcasted_iota(jnp.int32, (rows, LANES), 1)
     row = lax.broadcasted_iota(jnp.int32, (rows, LANES), 0)
     position = row * LANES + lane
-    out_ref[...] = jnp.full((rows, LANES), -1, jnp.int32)
+    out_ref[...] = jnp.full((rows, LANES), blank, jnp.int32)
     first = me_ref[0] * size
 
     def source(s, start):
@@ -109,7 +109,24 @@
     return arrived
 
 
-def table_kernel(groups, owners, shard_ref, out_ref, dict_send, dict_recv, send, recv, local):
+def table_kernel(
+    groups,
+    owners,
+    shard_ref,
+    zeros_ref,
+    codes_ref,
+    out_ref,
+    everyone_ref,
+    dict_send,
+    dict_recv,
+    send,
+    recv,
+    code_dict_send,
+    code_dict_recv,
+    code_send,
+    code_recv,
+    local,
+):
     r = lax.axis_index("rows")
     z = lax.axis_index("dict")
     shard = shard_ref.shape[0]
@@ -144,6 +161,50 @@
 
     nearest = sorted(range(1, owners), key=lambda d: min(d, owners - d))
     sent = []
+
+    def to(src, dst, send_sem, recv_sem, peer):
+        copy = pltpu.make_async_remote_copy(
+            src_ref=src,
+            dst_ref=dst,
+            send_sem=send_sem,
+            recv_sem=recv_sem,
+            device_id=peer,
+            device_id_type=pl.DeviceIdType.MESH,
+        )
+        copy.start()
+        sent.append(copy)
+        return copy
+
+    first = {}
+    mine = everyone_ref.at[r * owners + z]
+    code_first = {}
+    code_received = {}
+    code_order = orders[0]
+    code_stages = stages[0]
+
+    def forward_codes(src, d, offset, k):
+        owner = lax.rem(z + owners - d, owners)
+        dst = everyone_ref.at[flipped(r, offset) * owners + owner]
+        for later in range(k + 1, len(code_order)):
+            bit = code_order[later]
+            lane = d * groups + (offset ^ bit)
+            code_received[d, offset ^ bit] = to(
+                dst if src is None else src,
+                dst,
+                code_send.at[lane],
+                code_recv.at[lane],
+                plane(flipped(r, bit)),
+            )
+
+    for d in nearest:
+        code_first[d] = to(
+            codes_ref,
+            mine,
+            code_dict_send.at[d - 1],
+            code_dict_recv.at[d - 1],
+            column(lax.rem(z + d, owners)),
+        )
+    forward_codes(codes_ref, 0, 0, -1)
     for d in nearest:
         copy = pltpu.make_async_remote_copy(
             src_ref=shard_ref.at[pl.ds(pl.multiple_of(r * part, part), part)],
@@ -155,13 +216,28 @@
         )
         copy.start()
         sent.append(copy)
+        first[d] = copy
     own = pltpu.make_async_copy(
         shard_ref, out_ref.at[pl.ds(pl.multiple_of(z * shard, shard), shard)], local.at[0]
     )
     own.start()
+    blank = pltpu.make_async_copy(
+        zeros_ref, out_ref.at[pl.ds(owners * shard, zeros_ref.shape[0])], local.at[1]
+    )
+    blank.start()
+    own_codes = pltpu.make_async_copy(codes_ref, mine, local.at[2])
+    own_codes.start()
 
     received = {}
-    first = {d: sent[i] for i, d in enumerate(nearest)}
+    for index, (offset, k) in enumerate(code_stages):
+        for d in [0] + nearest:
+            if index == 0:
+                if d == 0:
+                    continue
+                code_first[d].wait_recv()
+            else:
+                code_received[d, offset].wait_recv()
+            forward_codes(None, d, offset, k)
     for index in range(groups):
         for d in nearest:
             owner = lax.rem(z + owners - d, owners)
@@ -189,6 +265,8 @@
     for copy in sent:
         copy.wait_send()
     own.wait()
+    blank.wait()
+    own_codes.wait()
 
 
 def flipped(r, mask):
@@ -201,28 +279,38 @@
     return out
 
 
-def gathered_table(decoding_table):
+def gathered(decoding_table, compacted):
     groups = lax.axis_size("rows")
     owners = lax.axis_size("dict")
     shard, width = decoding_table.shape
     flights = (owners - 1) * 2 * groups
+    vmem = pl.BlockSpec(memory_space=pltpu.VMEM)
+    anywhere = pl.BlockSpec(memory_space=pl.ANY)
+    zeros = jnp.zeros((16, width), decoding_table.dtype)
     return pl.pallas_call(
         functools.partial(table_kernel, groups, owners),
-        out_shape=jax.ShapeDtypeStruct((owners * shard, width), decoding_table.dtype),
-        in_specs=[pl.BlockSpec(memory_space=pltpu.VMEM)],
-        out_specs=pl.BlockSpec(memory_space=pl.ANY),
+        out_shape=(
+            jax.ShapeDtypeStruct((owners * shard + 16, width), decoding_table.dtype),
+            jax.ShapeDtypeStruct((owners * groups,) + compacted.shape, compacted.dtype),
+        ),
+        in_specs=[vmem, vmem, vmem],
+        out_specs=(anywhere, anywhere),
         scratch_shapes=[
             pltpu.SemaphoreType.DMA((owners - 1,)),
             pltpu.SemaphoreType.DMA((owners - 1,)),
             pltpu.SemaphoreType.DMA((flights,)),
             pltpu.SemaphoreType.DMA((flights,)),
-            pltpu.SemaphoreType.DMA((1,)),
+            pltpu.SemaphoreType.DMA((owners - 1,)),
+            pltpu.SemaphoreType.DMA((owners - 1,)),
+            pltpu.SemaphoreType.DMA((owners * groups,)),
+            pltpu.SemaphoreType.DMA((owners * groups,)),
+            pltpu.SemaphoreType.DMA((3,)),
         ],
         compiler_params=pltpu.CompilerParams(collective_id=0, has_side_effects=True),
         cost_estimate=pl.CostEstimate(
             flops=0, bytes_accessed=16 * owners * shard * width, transcendentals=0
         ),
-    )(decoding_table)
+    )(decoding_table, zeros, compacted)
 
 
 def on_device(lookup_keys_per_record, filter_passed_flags, decoding_table):
@@ -232,25 +320,22 @@
     vmem = pl.BlockSpec(memory_space=pltpu.VMEM)
     smem = pl.BlockSpec(memory_space=pltpu.SMEM)
 
-    table = gathered_table(decoding_table)
-
     compacted = pl.pallas_call(
         compact_kernel,
         out_shape=jax.ShapeDtypeStruct((rows + 8, LANES), jnp.int32),
         in_specs=[vmem, vmem],
         out_specs=vmem,
     )(lookup_keys_per_record.reshape(rows, LANES), filter_passed_flags.reshape(rows, LANES))
-    everyone = lax.all_gather(compacted, ("rows", "dict"))
+    table, everyone = gathered(decoding_table, compacted)
     counts = everyone[:, rows, 0]
     me = lax.axis_index(("rows", "dict")).astype(jnp.int32).reshape(1)
     codes = pl.pallas_call(
-        pick_kernel,
+        functools.partial(pick_kernel, shard * lax.axis_size("dict")),
         out_shape=jax.ShapeDtypeStruct((rows, LANES), jnp.int32),
         in_specs=[smem, smem, vmem],
         out_specs=vmem,
     )(me, counts, everyone).reshape(rows_here)
-    picked = jnp.take(table, jnp.maximum(codes, 0), axis=0, mode="clip")
-    return jnp.where((codes >= 0)[:, None], picked, jnp.zeros_like(picked))
+    return table.at[codes].get(mode="promise_in_bounds")
 
 
 def solution(mesh):

time: 144 us -> 80.9 us (0.56)
  blocking collectives: 75.4 us -> 0 us
  Pallas kernels: 46.8 us -> 58.1 us
  local copies, waits for them, and re-layouts: 16.7 us -> 21.5 us
  other arithmetic: 4.33 us -> 0.74 us
    all_gather x1 -> x0, blocking collectives: 75.4 us -> none  [on_device(): everyone = lax.all_gather(compacted, ('rows', 'dict'))]
    pallas_call x2, Pallas kernels: 44.3 us -> 55.6 us  [the longest x1 53.3 us: gathered(): pl.pallas_call(functools.partial(table_kernel, groups, owners), out_shape...]
    gather x1, local copies, waits for them, and re-layouts: 15.5 us -> 18.8 us  [on_device(): return table.at[codes].get(mode='promise_in_bounds')]
    select_n x1, other arithmetic: 2.88 us -> 0.73 us  [on_device(): return table.at[codes].get(mode='promise_in_bounds')]
where the time goes in v3:
time: 80.9 us; the launch traced here: 80.4 us
  Pallas kernels  58.1 us (72%)
  local copies, waits for them, and re-layouts  21.5 us (27%)
    pallas_call x1, Pallas kernels, gathered(): pl.pallas_call(functools.partial(table_kernel, groups, owners), out_shape...  53.3 us
    gather x1, local copies, waits for them, and re-layouts, on_device(): return table.at[codes].get(mode='promise_in_bounds')  18.8 us
    pallas_call x1, Pallas kernels, on_device(): pl.pallas_call(compact_kernel, out_shape=jax.ShapeDtypeStruct((rows + 8,...  2.54 us
    pallas_call x1, Pallas kernels, on_device(): pl.pallas_call(functools.partial(pick_kernel, shard * lax.axis_size('dict...  2.28 us
    slice x1, local copies, waits for them, and re-layouts, on_device(): counts = everyone[:, rows, 0]  2.09 us

profile of v3, /device:TPU:0, one launch (start us, length us, event | category | flops | bytes accessed | tf_op | source)
XLA Modules:
  0.0 80.4 jit_solution(9323751470974677115)
XLA Ops:
  0.0 2.5 %shard_map.37.codes_ref = s32[40,128]{1,0:T(8,128)} custom-call(s32[32,128]{1,0:T(8,128)} %bitcast.7, s32[32,128]{1,0:T(8,128)} %bitcast.8), custom_call_target="tpu_custom_call" | custom-call | tf_op jit(solution)/shard_map/pallas_call | solution.py:323
  2.5 0.6 broadcast_in_dim.4.zeros_ref
  3.1 53.3 %shard_map.38 = (bf16[32784,128]{1,0:T(8,128)(2,1)}, s32[32,40,128]{2,1,0:T(8,128)}) custom-call(bf16[8192,128]{1,0:T(8,128)(2,1)} %shard_ref.1, bf16[16,128]{1,0:T(8,128)(2,1)} %broadcast_in_dim.4.zeros_ref, s32[40,128]{1,0:T(8,128)} %shard_map.37.codes_ref), custom_call_target="tpu_custom_call" | custom-call | bytes 67108864 | tf_op jit(solution)/shard_map/pallas_call | solution.py:290
  56.5 2.1 %slice_reduce_fusion.counts_ref = s32[32]{0:T(128)} fusion(s32[32,40,128]{2,1,0:T(8,128)} %get-tuple-element.8.codes_ref), kind=kLoop, calls=%fused_computation.2 | loop fusion | bytes 256 | tf_op jit(solution)/shard_map/slice | solution.py:330
  58.5 2.3 %shard_map.39 = s32[32,128]{1,0:T(8,128)} custom-call(s32[1]{0:T(128)} %bitcast.2.me_ref, s32[32]{0:T(128)} %slice_reduce_fusion.counts_ref, s32[32,40,128]{2,1,0:T(8,128)} %get-tuple-element.8.codes_ref), custom_call_target="tpu_custom_call" | custom-call | tf_op jit(solution)/shard_map/pallas_call | solution.py:332
  60.8 0.7 compare_select_fusion
  61.6 18.8 %gather_fusion = bf16[4096,128]{1,0:T(8,128)(2,1)} fusion(bf16[32784,128]{1,0:T(8,128)(2,1)} %get-tuple-element.7, s32[4096]{0:T(1024)S(1)} %broadcast_clamp_fusion), kind=kCustom, calls=%fused_computation | custom fusion | bytes 2113536 | tf_op jit(solution)/shard_map/gather | solution.py:338
  (1 shorter events, 0.0 us)

commit v4 on v3

--- a/solution.py
+++ b/solution.py
@@ -8,6 +8,7 @@
 from jax.sharding import PartitionSpec as P
 
 LANES = 128
+GRANT = 12 * 1024 * 1024
 
 
 def shifted_left(x, step, lane):
@@ -65,18 +66,24 @@
     out_ref[rows:, :] = total
 
 
-def pick_kernel(blank, me_ref, counts_ref, codes_ref, out_ref):
+def decode_kernel(
+    blank, me_ref, codes_ref, table_ref, out_ref, picked, tallies, rows_f32, counts, codes, sem
+):
     blocks = codes_ref.shape[0]
     rows = codes_ref.shape[1] - 8
     size = rows * LANES
     lane = lax.broadcasted_iota(jnp.int32, (rows, LANES), 1)
     row = lax.broadcasted_iota(jnp.int32, (rows, LANES), 0)
     position = row * LANES + lane
-    out_ref[...] = jnp.full((rows, LANES), blank, jnp.int32)
+    tallies[...] = codes_ref[:, rows, :]
+    copy = pltpu.make_async_copy(tallies, counts, sem.at[0])
+    copy.start()
+    picked[...] = jnp.full((rows, LANES), blank, jnp.int32)
     first = me_ref[0] * size
+    copy.wait()
 
     def source(s, start):
-        count = counts_ref[s]
+        count = counts[s, 0]
         begin = start - first
 
         @pl.when((begin < size) & (begin + count > 0))
@@ -86,15 +93,31 @@
             by_lane = lax.rem(shift, LANES)
             moved = pltpu.roll(codes_ref[s, :rows, :], by_row, 0)
             below = pltpu.roll(moved, 1, 0)
-            picked = jnp.where(
+            mine = jnp.where(
                 lane >= by_lane, pltpu.roll(moved, by_lane, 1), pltpu.roll(below, by_lane, 1)
             )
             inside = (position >= begin) & (position < begin + count)
-            out_ref[...] = jnp.where(inside, picked, out_ref[...])
+            picked[...] = jnp.where(inside, mine, picked[...])
 
         return start + count
 
     lax.fori_loop(0, blocks, source, jnp.int32(0))
+    copy = pltpu.make_async_copy(picked, codes, sem.at[1])
+    copy.start()
+    copy.wait()
+
+    @pl.loop(0, rows)
+    def _(i):
+        for j in range(LANES):
+            code = codes[i, j]
+            pair = table_ref[code >> 1].astype(jnp.float32)
+            odd = (code & 1) == 1
+            rows_f32[pl.ds(i * LANES + j, 1), :] = jnp.where(odd, pair[1:2], pair[0:1])
+
+    @pl.loop(0, rows)
+    def _(i):
+        block = pl.ds(pl.multiple_of(i * LANES, LANES), LANES)
+        out_ref[block, :] = rows_f32[block, :].astype(out_ref.dtype)
 
 
 def forwarding(groups):
@@ -229,15 +252,6 @@
     own_codes.start()
 
     received = {}
-    for index, (offset, k) in enumerate(code_stages):
-        for d in [0] + nearest:
-            if index == 0:
-                if d == 0:
-                    continue
-                code_first[d].wait_recv()
-            else:
-                code_received[d, offset].wait_recv()
-            forward_codes(None, d, offset, k)
     for index in range(groups):
         for d in nearest:
             owner = lax.rem(z + owners - d, owners)
@@ -262,6 +276,15 @@
                     copy.start()
                     sent.append(copy)
                     received[d, h, offset ^ bit] = copy
+        offset, k = code_stages[index]
+        for d in [0] + nearest:
+            if index == 0:
+                if d == 0:
+                    continue
+                code_first[d].wait_recv()
+            else:
+                code_received[d, offset].wait_recv()
+            forward_codes(None, d, offset, k)
     for copy in sent:
         copy.wait_send()
     own.wait()
@@ -306,7 +329,9 @@
             pltpu.SemaphoreType.DMA((owners * groups,)),
             pltpu.SemaphoreType.DMA((3,)),
         ],
-        compiler_params=pltpu.CompilerParams(collective_id=0, has_side_effects=True),
+        compiler_params=pltpu.CompilerParams(
+            collective_id=0, has_side_effects=True, vmem_limit_bytes=GRANT
+        ),
         cost_estimate=pl.CostEstimate(
             flops=0, bytes_accessed=16 * owners * shard * width, transcendentals=0
         ),
@@ -325,17 +350,27 @@
         out_shape=jax.ShapeDtypeStruct((rows + 8, LANES), jnp.int32),
         in_specs=[vmem, vmem],
         out_specs=vmem,
+        compiler_params=pltpu.CompilerParams(vmem_limit_bytes=GRANT),
     )(lookup_keys_per_record.reshape(rows, LANES), filter_passed_flags.reshape(rows, LANES))
     table, everyone = gathered(decoding_table, compacted)
-    counts = everyone[:, rows, 0]
     me = lax.axis_index(("rows", "dict")).astype(jnp.int32).reshape(1)
-    codes = pl.pallas_call(
-        functools.partial(pick_kernel, shard * lax.axis_size("dict")),
-        out_shape=jax.ShapeDtypeStruct((rows, LANES), jnp.int32),
-        in_specs=[smem, smem, vmem],
+    blank = shard * lax.axis_size("dict")
+    blocks = everyone.shape[0]
+    return pl.pallas_call(
+        functools.partial(decode_kernel, blank),
+        out_shape=jax.ShapeDtypeStruct((rows_here, width), decoding_table.dtype),
+        in_specs=[smem, vmem, vmem],
         out_specs=vmem,
-    )(me, counts, everyone).reshape(rows_here)
-    return table.at[codes].get(mode="promise_in_bounds")
+        scratch_shapes=[
+            pltpu.VMEM((rows, LANES), jnp.int32),
+            pltpu.VMEM((blocks, LANES), jnp.int32),
+            pltpu.VMEM((rows_here, width), jnp.float32),
+            pltpu.SMEM((blocks, LANES), jnp.int32),
+            pltpu.SMEM((rows, LANES), jnp.int32),
+            pltpu.SemaphoreType.DMA((2,)),
+        ],
+        compiler_params=pltpu.CompilerParams(vmem_limit_bytes=40 * 1024 * 1024),
+    )(me, everyone, table.reshape(table.shape[0] // 2, 2, width))
 
 
 def solution(mesh):

time: 80.9 us -> 65 us (0.80)
  local copies, waits for them, and re-layouts: 21.5 us -> 3.02 us
  Pallas kernels: 58.1 us -> 61.6 us
    gather x1 -> x0, local copies, waits for them, and re-layouts: 18.8 us -> none  [on_device(): return table.at[codes].get(mode='promise_in_bounds')]
    pallas_call x1, Pallas kernels: 2.28 us -> 9.16 us  [on_device(): pl.pallas_call(functools.partial(decode_kernel, blank), out_shape=jax.Sha...]
    unnamed x0 -> x6, local copies, waits for them, and re-layouts: none -> 3.02 us
    slice x1 -> x0, local copies, waits for them, and re-layouts: 2.09 us -> none  [on_device(): counts = everyone[:, rows, 0]]
    pallas_call x1, Pallas kernels: 53.3 us -> 51.3 us  [gathered(): pl.pallas_call(functools.partial(table_kernel, groups, owners), out_shape...]
    pallas_call x1, Pallas kernels: 2.54 us -> 1.2 us  [on_device(): pl.pallas_call(compact_kernel, out_shape=jax.ShapeDtypeStruct((rows + 8,...]
where the time goes in v4:
time: 65 us; the launch traced here: 64.7 us
  Pallas kernels  61.6 us (95%)
  local copies, waits for them, and re-layouts  3.02 us (5%)
    pallas_call x1, Pallas kernels, gathered(): pl.pallas_call(functools.partial(table_kernel, groups, owners), out_shape...  51.3 us
    pallas_call x1, Pallas kernels, on_device(): pl.pallas_call(functools.partial(decode_kernel, blank), out_shape=jax.Sha...  9.16 us
    unnamed x6, local copies, waits for them, and re-layouts  3.02 us

profile of v4, /device:TPU:0, one launch (start us, length us, event | category | flops | bytes accessed | tf_op | source)
XLA Modules:
  0.0 64.7 jit_solution(8515277585325523397)
XLA Ops:
  0.0 0.0 copy-start.1
  0.0 0.7 %copy-done.1 = s32[4096]{0:T(1024)S(1)} copy-done((s32[4096]{0:T(1024)S(1)}, s32[4096]{0:T(1024)}, u32[]{:S(2)}) %copy-start.1) | copy-done | bytes 16408
  0.7 0.0 copy-start.2
  0.7 0.7 %copy-done.2 = s32[4096]{0:T(1024)S(1)} copy-done((s32[4096]{0:T(1024)S(1)}, s32[4096]{0:T(1024)}, u32[]{:S(2)}) %copy-start.2) | copy-done | bytes 16408
  1.4 1.2 %shard_map.37.codes_ref = s32[40,128]{1,0:T(8,128)S(1)} custom-call(s32[32,128]{1,0:T(8,128)S(1)} %bitcast.5, s32[32,128]{1,0:T(8,128)S(1)} %bitcast.6), custom_call_target="tpu_custom_call" | custom-call | tf_op jit(solution)/shard_map/pallas_call | solution.py:348
  2.7 0.0 copy-start
  2.7 1.6 %copy-done = bf16[8192,128]{1,0:T(8,128)(2,1)S(1)} copy-done((bf16[8192,128]{1,0:T(8,128)(2,1)S(1)}, bf16[8192,128]{1,0:T(8,128)(2,1)}, u32[]{:S(2)}) %copy-start) | copy-done | bytes 2097176
  4.3 51.3 %shard_map.38 = (bf16[32784,128]{1,0:T(8,128)(2,1)S(1)}, s32[32,40,128]{2,1,0:T(8,128)S(1)}) custom-call(bf16[8192,128]{1,0:T(8,128)(2,1)S(1)} %copy-done, bf16[16,128]{1,0:T(8,128)(2,1)S(1)} %broadcast_in_dim.3.zeros_ref, s32[40,128]{1,0:T(8,128)S(1)} %shard_map.37.codes_ref), custom_call_target="tpu_custom_call" | custom-call | bytes 67108864 | tf_op jit(solution)/shard_map/pallas_call | solution.py:313
  55.5 9.2 %shard_map.39 = bf16[4096,128]{1,0:T(8,128)(2,1)} custom-call(s32[1]{0:T(128)} %bitcast.me_ref, s32[32,40,128]{2,1,0:T(8,128)S(1)} %get-tuple-element.7.codes_ref, bf16[16392,2,128]{2,1,0:T(2,128)(2,1)S(1)} %bitcast.4), custom_call_target="tpu_custom_call" | custom-call | tf_op jit(solution)/shard_map/pallas_call | solution.py:359
  (1 shorter events, 0.0 us)
Async XLA Ops:
  0.0 0.7 %copy-start.1 = (s32[4096]{0:T(1024)S(1)}, s32[4096]{0:T(1024)}, u32[]{:S(2)}) copy-start(s32[4096]{0:T(1024)} %param.3) | copy-start | bytes 49156
  0.7 0.7 %copy-start.2 = (s32[4096]{0:T(1024)S(1)}, s32[4096]{0:T(1024)}, u32[]{:S(2)}) copy-start(s32[4096]{0:T(1024)} %param.4) | copy-start | bytes 49156
  2.7 1.6 %copy-start = (bf16[8192,128]{1,0:T(8,128)(2,1)S(1)}, bf16[8192,128]{1,0:T(8,128)(2,1)}, u32[]{:S(2)}) copy-start(bf16[8192,128]{1,0:T(8,128)(2,1)} %shard_ref.1) | copy-start | bytes 6291460

commit v5 on v4

--- a/solution.py
+++ b/solution.py
@@ -182,11 +182,10 @@
         at = owner * shard + group * part + start
         return pl.ds(pl.multiple_of(at, half), size)
 
-    nearest = sorted(range(1, owners), key=lambda d: min(d, owners - d))
     sent = []
 
     def to(src, dst, send_sem, recv_sem, peer):
-        copy = pltpu.make_async_remote_copy(
+        return pltpu.make_async_remote_copy(
             src_ref=src,
             dst_ref=dst,
             send_sem=send_sem,
@@ -194,52 +193,68 @@
             device_id=peer,
             device_id_type=pl.DeviceIdType.MESH,
         )
-        copy.start()
-        sent.append(copy)
-        return copy
-
-    first = {}
+
+    def relay(src, owner, d, h, upward):
+        arrives_as = d + 1 if upward else lax.rem(d + owners - 1, owners)
+        lane = arrives_as * 2 + h
+        peer = lax.rem(z + (1 if upward else owners - 1), owners)
+        return to(
+            src,
+            out_ref.at[place(owner, r, h * half, half)],
+            dict_send.at[lane + (0 if upward else 2 * owners)],
+            dict_recv.at[lane],
+            column(peer),
+        )
+
+    relayed = []
+
+    def relay_if(wanted, *where):
+        @pl.when(wanted)
+        def _():
+            relay(*where).start()
+
+        relayed.append((wanted, where))
+
     mine = everyone_ref.at[r * owners + z]
     code_first = {}
     code_received = {}
-    code_order = orders[0]
-    code_stages = stages[0]
 
     def forward_codes(src, d, offset, k):
         owner = lax.rem(z + owners - d, owners)
         dst = everyone_ref.at[flipped(r, offset) * owners + owner]
-        for later in range(k + 1, len(code_order)):
-            bit = code_order[later]
+        order = orders[d % 2]
+        for later in range(k + 1, len(order)):
+            bit = order[later]
             lane = d * groups + (offset ^ bit)
-            code_received[d, offset ^ bit] = to(
+            copy = to(
                 dst if src is None else src,
                 dst,
                 code_send.at[lane],
                 code_recv.at[lane],
                 plane(flipped(r, bit)),
             )
-
-    for d in nearest:
-        code_first[d] = to(
+            copy.start()
+            sent.append(copy)
+            code_received[d, offset ^ bit] = copy
+
+    def own_half(h):
+        return shard_ref.at[pl.ds(pl.multiple_of(r * part + h * half, half), half)]
+
+    for h in range(2):
+        relay_if(z + 1 < owners, own_half(h), z, 0, h, True)
+        relay_if(z > 0, own_half(h), z, 0, h, False)
+    for d in range(1, owners):
+        copy = to(
             codes_ref,
             mine,
             code_dict_send.at[d - 1],
             code_dict_recv.at[d - 1],
             column(lax.rem(z + d, owners)),
         )
-    forward_codes(codes_ref, 0, 0, -1)
-    for d in nearest:
-        copy = pltpu.make_async_remote_copy(
-            src_ref=shard_ref.at[pl.ds(pl.multiple_of(r * part, part), part)],
-            dst_ref=out_ref.at[place(z, r, 0, part)],
-            send_sem=dict_send.at[d - 1],
-            recv_sem=dict_recv.at[d - 1],
-            device_id=column(lax.rem(z + d, owners)),
-            device_id_type=pl.DeviceIdType.MESH,
-        )
         copy.start()
         sent.append(copy)
-        first[d] = copy
+        code_first[d] = copy
+    forward_codes(codes_ref, 0, 0, -1)
     own = pltpu.make_async_copy(
         shard_ref, out_ref.at[pl.ds(pl.multiple_of(z * shard, shard), shard)], local.at[0]
     )
@@ -251,42 +266,82 @@
     own_codes = pltpu.make_async_copy(codes_ref, mine, local.at[2])
     own_codes.start()
 
+    both = jnp.minimum(z, owners - 1 - z)
+    longer_below = z > owners - 1 - z
+
+    def arrival(i):
+        paired = i < 2 * both
+        distance = jnp.where(paired, i // 2 + 1, i - both + 1)
+        if i % 2 == 0:
+            below = paired | longer_below
+        else:
+            below = jnp.logical_not(paired) & longer_below
+        d = jnp.where(below, distance, owners - distance)
+        return d, below
+
     received = {}
-    for index in range(groups):
-        for d in nearest:
-            owner = lax.rem(z + owners - d, owners)
-            if index == 0:
-                first[d].wait_recv()
+
+    def forward(i, d, h, index):
+        owner = lax.rem(z + owners - d, owners)
+        offset, k = stages[h][index]
+        where = place(owner, flipped(r, offset), h * half, half)
+        for later in range(k + 1, len(orders[h])):
+            bit = orders[h][later]
+            lane = (i * 2 + h) * groups + (offset ^ bit)
+            copy = to(
+                out_ref.at[where],
+                out_ref.at[where],
+                send.at[lane],
+                recv.at[lane],
+                plane(flipped(r, bit)),
+            )
+            copy.start()
+            sent.append(copy)
+            received[i, h, offset ^ bit] = copy
+
+    def plane_step(i, first, last):
+        for index in range(first, last):
             for h in range(2):
-                offset, k = stages[h][index]
-                if index > 0:
-                    received[d, h, offset].wait_recv()
-                where = place(owner, flipped(r, offset), h * half, half)
-                for later in range(k + 1, len(orders[h])):
-                    bit = orders[h][later]
-                    lane = ((d - 1) * 2 + h) * groups + (offset ^ bit)
-                    copy = pltpu.make_async_remote_copy(
-                        src_ref=out_ref.at[where],
-                        dst_ref=out_ref.at[where],
-                        send_sem=send.at[lane],
-                        recv_sem=recv.at[lane],
-                        device_id=plane(flipped(r, bit)),
-                        device_id_type=pl.DeviceIdType.MESH,
-                    )
-                    copy.start()
-                    sent.append(copy)
-                    received[d, h, offset ^ bit] = copy
-        offset, k = code_stages[index]
-        for d in [0] + nearest:
-            if index == 0:
-                if d == 0:
-                    continue
+                received[i, h, stages[h][index][0]].wait_recv()
+                forward(i, arrival(i)[0], h, index)
+
+    def code_step(index):
+        for d in range(owners):
+            offset, k = stages[d % 2][index]
+            if index > 0:
+                code_received[d, offset].wait_recv()
+            elif d > 0:
                 code_first[d].wait_recv()
             else:
-                code_received[d, offset].wait_recv()
+                continue
             forward_codes(None, d, offset, k)
+
+    for i in range(owners - 1):
+        d, below = arrival(i)
+        owner = lax.rem(z + owners - d, owners)
+        for h in range(2):
+            spot = out_ref.at[place(owner, r, h * half, half)]
+            to(spot, spot, dict_send.at[0], dict_recv.at[d * 2 + h], column(owner)).wait_recv()
+            relay_if(below & (z + 1 < owners), spot, owner, d, h, True)
+            relay_if(jnp.logical_not(below) & (z > 0), spot, owner, d, h, False)
+            forward(i, d, h, 0)
+        if i > 0:
+            plane_step(i - 1, 1, groups // 2)
+        if i < groups:
+            code_step(i)
+    plane_step(owners - 2, 1, groups // 2)
+    for index in range(owners - 1, groups):
+        code_step(index)
+    for i in range(owners - 1):
+        plane_step(i, groups // 2, groups)
     for copy in sent:
         copy.wait_send()
+    for wanted, where in relayed:
+
+        @pl.when(wanted)
+        def _():
+            relay(*where).wait_send()
+
     own.wait()
     blank.wait()
     own_codes.wait()
@@ -319,8 +374,8 @@
         in_specs=[vmem, vmem, vmem],
         out_specs=(anywhere, anywhere),
         scratch_shapes=[
-            pltpu.SemaphoreType.DMA((owners - 1,)),
-            pltpu.SemaphoreType.DMA((owners - 1,)),
+            pltpu.SemaphoreType.DMA((4 * owners,)),
+            pltpu.SemaphoreType.DMA((2 * owners,)),
             pltpu.SemaphoreType.DMA((flights,)),
             pltpu.SemaphoreType.DMA((flights,)),
             pltpu.SemaphoreType.DMA((owners - 1,)),

time: 65 us -> 61.6 us (0.948)
  Pallas kernels: 61.6 us -> 58 us
    pallas_call x1, Pallas kernels: 51.3 us -> 47.7 us  [gathered(): pl.pallas_call(functools.partial(table_kernel, groups, owners), out_shape...]
where the time goes in v5:
time: 61.6 us; the launch traced here: 61 us
  Pallas kernels  58 us (94%)
  local copies, waits for them, and re-layouts  3.02 us (5%)
    pallas_call x1, Pallas kernels, gathered(): pl.pallas_call(functools.partial(table_kernel, groups, owners), out_shape...  47.7 us
    pallas_call x1, Pallas kernels, on_device(): pl.pallas_call(functools.partial(decode_kernel, blank), out_shape=jax.Sha...  9.09 us
    unnamed x6, local copies, waits for them, and re-layouts  3.02 us

profile of v5, /device:TPU:0, one launch (start us, length us, event | category | flops | bytes accessed | tf_op | source)
XLA Modules:
  0.0 61.0 jit_solution(8572517588953291331)
XLA Ops:
  0.0 0.0 copy-start.1
  0.0 0.7 %copy-done.1 = s32[4096]{0:T(1024)S(1)} copy-done((s32[4096]{0:T(1024)S(1)}, s32[4096]{0:T(1024)}, u32[]{:S(2)}) %copy-start.1) | copy-done | bytes 16408
  0.7 0.0 copy-start.2
  0.7 0.7 %copy-done.2 = s32[4096]{0:T(1024)S(1)} copy-done((s32[4096]{0:T(1024)S(1)}, s32[4096]{0:T(1024)}, u32[]{:S(2)}) %copy-start.2) | copy-done | bytes 16408
  1.4 1.2 %shard_map.37.codes_ref = s32[40,128]{1,0:T(8,128)S(1)} custom-call(s32[32,128]{1,0:T(8,128)S(1)} %bitcast.5, s32[32,128]{1,0:T(8,128)S(1)} %bitcast.6), custom_call_target="tpu_custom_call" | custom-call | tf_op jit(solution)/shard_map/pallas_call | solution.py:403
  2.7 0.0 copy-start
  2.7 1.6 %copy-done = bf16[8192,128]{1,0:T(8,128)(2,1)S(1)} copy-done((bf16[8192,128]{1,0:T(8,128)(2,1)S(1)}, bf16[8192,128]{1,0:T(8,128)(2,1)}, u32[]{:S(2)}) %copy-start) | copy-done | bytes 2097176
  4.3 47.7 %shard_map.38 = (bf16[32784,128]{1,0:T(8,128)(2,1)S(1)}, s32[32,40,128]{2,1,0:T(8,128)S(1)}) custom-call(bf16[8192,128]{1,0:T(8,128)(2,1)S(1)} %copy-done, bf16[16,128]{1,0:T(8,128)(2,1)S(1)} %broadcast_in_dim.3.zeros_ref, s32[40,128]{1,0:T(8,128)S(1)} %shard_map.37.codes_ref), custom_call_target="tpu_custom_call" | custom-call | bytes 67108864 | tf_op jit(solution)/shard_map/pallas_call | solution.py:368
  52.0 9.1 %shard_map.39 = bf16[4096,128]{1,0:T(8,128)(2,1)} custom-call(s32[1]{0:T(128)} %bitcast.me_ref, s32[32,40,128]{2,1,0:T(8,128)S(1)} %get-tuple-element.7.codes_ref, bf16[16392,2,128]{2,1,0:T(2,128)(2,1)S(1)} %bitcast.4), custom_call_target="tpu_custom_call" | custom-call | tf_op jit(solution)/shard_map/pallas_call | solution.py:414
  (1 shorter events, 0.0 us)
Async XLA Ops:
  0.0 0.7 %copy-start.1 = (s32[4096]{0:T(1024)S(1)}, s32[4096]{0:T(1024)}, u32[]{:S(2)}) copy-start(s32[4096]{0:T(1024)} %param.3) | copy-start | bytes 49156
  0.7 0.7 %copy-start.2 = (s32[4096]{0:T(1024)S(1)}, s32[4096]{0:T(1024)}, u32[]{:S(2)}) copy-start(s32[4096]{0:T(1024)} %param.4) | copy-start | bytes 49156
  2.7 1.6 %copy-start = (bf16[8192,128]{1,0:T(8,128)(2,1)S(1)}, bf16[8192,128]{1,0:T(8,128)(2,1)}, u32[]{:S(2)}) copy-start(bf16[8192,128]{1,0:T(8,128)(2,1)} %shard_ref.1) | copy-start | bytes 6291460

commit v6 on v5

--- a/solution.py
+++ b/solution.py
@@ -240,9 +240,6 @@
     def own_half(h):
         return shard_ref.at[pl.ds(pl.multiple_of(r * part + h * half, half), half)]
 
-    for h in range(2):
-        relay_if(z + 1 < owners, own_half(h), z, 0, h, True)
-        relay_if(z > 0, own_half(h), z, 0, h, False)
     for d in range(1, owners):
         copy = to(
             codes_ref,
@@ -255,6 +252,9 @@
         sent.append(copy)
         code_first[d] = copy
     forward_codes(codes_ref, 0, 0, -1)
+    for h in range(2):
+        relay_if(z + 1 < owners, own_half(h), z, 0, h, True)
+        relay_if(z > 0, own_half(h), z, 0, h, False)
     own = pltpu.make_async_copy(
         shard_ref, out_ref.at[pl.ds(pl.multiple_of(z * shard, shard), shard)], local.at[0]
     )
@@ -316,6 +316,7 @@
                 continue
             forward_codes(None, d, offset, k)
 
+    code_step(0)
     for i in range(owners - 1):
         d, below = arrival(i)
         owner = lax.rem(z + owners - d, owners)
@@ -327,10 +328,13 @@
             forward(i, d, h, 0)
         if i > 0:
             plane_step(i - 1, 1, groups // 2)
-        if i < groups:
-            code_step(i)
+        if i == 0:
+            code_step(1)
+        if i == 1:
+            for index in range(2, groups // 2):
+                code_step(index)
     plane_step(owners - 2, 1, groups // 2)
-    for index in range(owners - 1, groups):
+    for index in range(groups // 2, groups):
         code_step(index)
     for i in range(owners - 1):
         plane_step(i, groups // 2, groups)

time: 61.6 us -> 62.4 us (1.013)
  Pallas kernels: 58 us -> 58.8 us
    pallas_call x1, Pallas kernels: 47.7 us -> 48.5 us  [gathered(): pl.pallas_call(functools.partial(table_kernel, groups, owners), out_shape...]
where the time goes in v6:
time: 62.4 us; the launch traced here: 61.8 us
  Pallas kernels  58.8 us (94%)
  local copies, waits for them, and re-layouts  3.02 us (5%)
    pallas_call x1, Pallas kernels, gathered(): pl.pallas_call(functools.partial(table_kernel, groups, owners), out_shape...  48.5 us
    pallas_call x1, Pallas kernels, on_device(): pl.pallas_call(functools.partial(decode_kernel, blank), out_shape=jax.Sha...  9.09 us
    unnamed x6, local copies, waits for them, and re-layouts  3.02 us

profile of v6, /device:TPU:0, one launch (start us, length us, event | category | flops | bytes accessed | tf_op | source)
XLA Modules:
  0.0 61.8 jit_solution(2092453234178934381)
XLA Ops:
  0.0 0.0 copy-start.1
  0.0 0.7 %copy-done.1 = s32[4096]{0:T(1024)S(1)} copy-done((s32[4096]{0:T(1024)S(1)}, s32[4096]{0:T(1024)}, u32[]{:S(2)}) %copy-start.1) | copy-done | bytes 16408
  0.7 0.0 copy-start.2
  0.7 0.7 %copy-done.2 = s32[4096]{0:T(1024)S(1)} copy-done((s32[4096]{0:T(1024)S(1)}, s32[4096]{0:T(1024)}, u32[]{:S(2)}) %copy-start.2) | copy-done | bytes 16408
  1.4 1.2 %shard_map.37.codes_ref = s32[40,128]{1,0:T(8,128)S(1)} custom-call(s32[32,128]{1,0:T(8,128)S(1)} %bitcast.5, s32[32,128]{1,0:T(8,128)S(1)} %bitcast.6), custom_call_target="tpu_custom_call" | custom-call | tf_op jit(solution)/shard_map/pallas_call | solution.py:407
  2.7 0.0 copy-start
  2.7 1.6 %copy-done = bf16[8192,128]{1,0:T(8,128)(2,1)S(1)} copy-done((bf16[8192,128]{1,0:T(8,128)(2,1)S(1)}, bf16[8192,128]{1,0:T(8,128)(2,1)}, u32[]{:S(2)}) %copy-start) | copy-done | bytes 2097176
  4.3 48.5 %shard_map.38 = (bf16[32784,128]{1,0:T(8,128)(2,1)S(1)}, s32[32,40,128]{2,1,0:T(8,128)S(1)}) custom-call(bf16[8192,128]{1,0:T(8,128)(2,1)S(1)} %copy-done, bf16[16,128]{1,0:T(8,128)(2,1)S(1)} %broadcast_in_dim.3.zeros_ref, s32[40,128]{1,0:T(8,128)S(1)} %shard_map.37.codes_ref), custom_call_target="tpu_custom_call" | custom-call | bytes 67108864 | tf_op jit(solution)/shard_map/pallas_call | solution.py:372
  52.7 9.1 %shard_map.39 = bf16[4096,128]{1,0:T(8,128)(2,1)} custom-call(s32[1]{0:T(128)} %bitcast.me_ref, s32[32,40,128]{2,1,0:T(8,128)S(1)} %get-tuple-element.7.codes_ref, bf16[16392,2,128]{2,1,0:T(2,128)(2,1)S(1)} %bitcast.4), custom_call_target="tpu_custom_call" | custom-call | tf_op jit(solution)/shard_map/pallas_call | solution.py:418
  (1 shorter events, 0.0 us)
Async XLA Ops:
  0.0 0.7 %copy-start.1 = (s32[4096]{0:T(1024)S(1)}, s32[4096]{0:T(1024)}, u32[]{:S(2)}) copy-start(s32[4096]{0:T(1024)} %param.3) | copy-start | bytes 49156
  0.7 0.7 %copy-start.2 = (s32[4096]{0:T(1024)S(1)}, s32[4096]{0:T(1024)}, u32[]{:S(2)}) copy-start(s32[4096]{0:T(1024)} %param.4) | copy-start | bytes 49156
  2.7 1.6 %copy-start = (bf16[8192,128]{1,0:T(8,128)(2,1)S(1)}, bf16[8192,128]{1,0:T(8,128)(2,1)}, u32[]{:S(2)}) copy-start(bf16[8192,128]{1,0:T(8,128)(2,1)} %shard_ref.1) | copy-start | bytes 6291460

commit v7 on v5

--- a/solution.py
+++ b/solution.py
@@ -258,7 +258,6 @@
     own = pltpu.make_async_copy(
         shard_ref, out_ref.at[pl.ds(pl.multiple_of(z * shard, shard), shard)], local.at[0]
     )
-    own.start()
     blank = pltpu.make_async_copy(
         zeros_ref, out_ref.at[pl.ds(owners * shard, zeros_ref.shape[0])], local.at[1]
     )
@@ -325,6 +324,8 @@
             relay_if(below & (z + 1 < owners), spot, owner, d, h, True)
             relay_if(jnp.logical_not(below) & (z > 0), spot, owner, d, h, False)
             forward(i, d, h, 0)
+        if i == 0:
+            own.start()
         if i > 0:
             plane_step(i - 1, 1, groups // 2)
         if i < groups:
@@ -371,7 +372,7 @@
             jax.ShapeDtypeStruct((owners * shard + 16, width), decoding_table.dtype),
             jax.ShapeDtypeStruct((owners * groups,) + compacted.shape, compacted.dtype),
         ),
-        in_specs=[vmem, vmem, vmem],
+        in_specs=[pl.BlockSpec(memory_space=pltpu.HBM), vmem, vmem],
         out_specs=(anywhere, anywhere),
         scratch_shapes=[
             pltpu.SemaphoreType.DMA((4 * owners,)),

time: 61.6 us -> 61.6 us (level)
  no operation moved by 1% of the time
where the time goes in v7:
time: 61.6 us; the launch traced here: 61.1 us
  Pallas kernels  58.1 us (94%)
  local copies, waits for them, and re-layouts  3.02 us (5%)
    pallas_call x1, Pallas kernels, gathered(): pl.pallas_call(functools.partial(table_kernel, groups, owners), out_shape...  47.7 us
    pallas_call x1, Pallas kernels, on_device(): pl.pallas_call(functools.partial(decode_kernel, blank), out_shape=jax.Sha...  9.16 us
    unnamed x6, local copies, waits for them, and re-layouts  3.02 us

profile of v7, /device:TPU:0, one launch (start us, length us, event | category | flops | bytes accessed | tf_op | source)
XLA Modules:
  0.0 61.1 jit_solution(10288188931781846379)
XLA Ops:
  0.0 0.0 copy-start.1
  0.0 0.7 %copy-done.1 = s32[4096]{0:T(1024)S(1)} copy-done((s32[4096]{0:T(1024)S(1)}, s32[4096]{0:T(1024)}, u32[]{:S(2)}) %copy-start.1) | copy-done | bytes 16408
  0.7 0.0 copy-start.2
  0.7 0.7 %copy-done.2 = s32[4096]{0:T(1024)S(1)} copy-done((s32[4096]{0:T(1024)S(1)}, s32[4096]{0:T(1024)}, u32[]{:S(2)}) %copy-start.2) | copy-done | bytes 16408
  1.4 1.2 %shard_map.37.codes_ref = s32[40,128]{1,0:T(8,128)S(1)} custom-call(s32[32,128]{1,0:T(8,128)S(1)} %bitcast.5, s32[32,128]{1,0:T(8,128)S(1)} %bitcast.6), custom_call_target="tpu_custom_call" | custom-call | tf_op jit(solution)/shard_map/pallas_call | solution.py:404
  2.7 0.0 copy-start
  2.7 1.6 %copy-done = bf16[8192,128]{1,0:T(8,128)(2,1)S(1)} copy-done((bf16[8192,128]{1,0:T(8,128)(2,1)S(1)}, bf16[8192,128]{1,0:T(8,128)(2,1)}, u32[]{:S(2)}) %copy-start) | copy-done | bytes 2097176
  4.3 47.7 %shard_map.38 = (bf16[32784,128]{1,0:T(8,128)(2,1)S(1)}, s32[32,40,128]{2,1,0:T(8,128)S(1)}) custom-call(bf16[8192,128]{1,0:T(8,128)(2,1)S(1)} %copy-done, bf16[16,128]{1,0:T(8,128)(2,1)S(1)} %broadcast_in_dim.3.zeros_ref, s32[40,128]{1,0:T(8,128)S(1)} %shard_map.37.codes_ref), custom_call_target="tpu_custom_call" | custom-call | bytes 67108864 | tf_op jit(solution)/shard_map/pallas_call | solution.py:369
  52.0 9.2 %shard_map.39 = bf16[4096,128]{1,0:T(8,128)(2,1)} custom-call(s32[1]{0:T(128)} %bitcast.me_ref, s32[32,40,128]{2,1,0:T(8,128)S(1)} %get-tuple-element.7.codes_ref, bf16[16392,2,128]{2,1,0:T(2,128)(2,1)S(1)} %bitcast.4), custom_call_target="tpu_custom_call" | custom-call | tf_op jit(solution)/shard_map/pallas_call | solution.py:415
  (1 shorter events, 0.0 us)
Async XLA Ops:
  0.0 0.7 %copy-start.1 = (s32[4096]{0:T(1024)S(1)}, s32[4096]{0:T(1024)}, u32[]{:S(2)}) copy-start(s32[4096]{0:T(1024)} %param.3) | copy-start | bytes 49156
  0.7 0.7 %copy-start.2 = (s32[4096]{0:T(1024)S(1)}, s32[4096]{0:T(1024)}, u32[]{:S(2)}) copy-start(s32[4096]{0:T(1024)} %param.4) | copy-start | bytes 49156
  2.7 1.6 %copy-start = (bf16[8192,128]{1,0:T(8,128)(2,1)S(1)}, bf16[8192,128]{1,0:T(8,128)(2,1)}, u32[]{:S(2)}) copy-start(bf16[8192,128]{1,0:T(8,128)(2,1)} %shard_ref.1) | copy-start | bytes 6291460
